TPU v7x, 256 devices: a whole 4x4x8 slice. The times are simulated.
256 devices in a mesh: dom: 64 (over z, x, core), inst: 4 (over y).
Axes of the slice: x: 4, y: 4, z: 8, core: 2. Of those that a mesh axis runs over, the one named last changes fastest.
Arguments:
- state: float32 [5, 16, 32768], P(None, 'inst', 'dom'), may hold values from -0.65 to 3.75, as said below
- cell_volume: float32 [32768], P('dom'), may hold values from 1 to 4
- step_size: float32 [32768], P('dom'), may hold values from 0.02 to 0.1
- face_normal: float32 [3, 131072], P(None, 'dom'), may hold values from -1 to 1
- owner_arm: float32 [3, 131072], P(None, 'dom'), may hold values from -0.09 to 0.09
- neighbor_arm: float32 [3, 131072], P(None, 'dom'), may hold values from -0.09 to 0.09
- face_owner: int32 [131072], P('dom'), may hold values from 0 to 511, as said below
- face_neighbor: int32 [131072], P('dom'), may hold values from 0 to 767, as said below
- face_count: int32 [64], P('dom'), may hold values from 1024 to 2048, as said below
- send_cells: int32 [256, 64], P('dom'), may hold values from 0 to 511
Outputs:
- new_state: float32 [5, 16, 32768], P(None, 'inst', 'dom')
- residual: float32 [5, 16, 32768], P(None, 'inst', 'dom')
Inputs may be any that keep to these rules, and one draw needn't show every extreme that they name: The state is physical: density 0.7 to 1.3 and pressure 0.4 (E - |m|^2 / (2 rho)) 0.7 to 1.3. `face_owner`: local ids of cells of the face's own partition. `face_neighbor`: either a local cell id below 512, or the ghost id 512 + k * 64 + s of block k; blocks of partitions that do not exist are never named. `face_count`: live face slots come first in each partition; some partition has all 2048 slots live. `send_cells`: row 4 q + k lists cells of partition q that fill ghost block k of partition q - o_k, o = (-2, -1, 1, 2); slots that no face names are padding.
All inputs are finite; a program needn't handle non-finite values.
Results may differ from a plain program's by a relative error of at most 0.0003.
Values sent between devices are 32-bit elements; how exact they have to be, the bound alone decides.
No kernel may reach another device: no remote copies, remote signals or barrier semaphores. Data moves between devices by JAX's collectives and lax.ppermute only.
A program may use at most 128 MiB of HBM per device.

v0:
```python
import functools

import jax
import jax.numpy as jnp
import numpy as np
from jax import lax
from jax.experimental import pallas as pl
from jax.experimental.pallas import tpu as pltpu
from jax.sharding import PartitionSpec as P

HEAT_RATIO = 1.4
FREQUENCY = 0.5
NV = 5
CELLS = 512
GHOSTS = 256
FACES = 2048
CHUNK = 512
VROWS = 40
GROWS = 120
BF = jnp.bfloat16
F32 = jnp.float32


def top_rows(shape):
    return (lax.broadcasted_iota(jnp.int32, shape, 0) & 7) < 4


def swap_halves(x):
    return pltpu.roll(x, 4, 0)


def fold(x):
    return x + swap_halves(x)


def pieces(x):
    high = x.astype(BF).astype(F32)
    return jnp.where(top_rows(x.shape), high, x - high).astype(BF)


def matmul(a, b):
    return jnp.dot(a, b, preferred_element_type=F32)


def matmul_t(a, b):
    return lax.dot_general(a, b, (((1,), (1,)), ((), ())), preferred_element_type=F32)


def one_hot(ids, rows):
    cell = lax.broadcasted_iota(jnp.int32, (rows, ids.shape[1]), 0)
    return jnp.where(cell == ids, 1.0, 0.0).astype(F32)


def paired(groups):
    out = []
    for j in range(0, len(groups), 2):
        first = groups[j]
        second = groups[min(j + 1, len(groups) - 1)]
        out.append(jnp.where(top_rows(first.shape), first, second))
    return jnp.concatenate(out, axis=0)


def unpaired(x, count):
    out = []
    for g in range(count):
        block = x[(g // 2) * 8 : (g // 2) * 8 + 8]
        turned = swap_halves(block)
        top = top_rows(block.shape)
        out.append(jnp.where(top, block, turned) if g % 2 == 0 else jnp.where(top, turned, block))
    return jnp.concatenate(out, axis=0)


def send_hot(send):
    return jnp.concatenate([one_hot(send[k : k + 1, :], CELLS) for k in range(4)], axis=1).astype(BF)


def write_messages(table, send, parity, near_ref, far_ref):
    listed = matmul(table, send_hot(send))
    groups = [fold(listed[8 * g : 8 * g + 8]) for g in range(listed.shape[0] // 8)]
    packed = paired(groups)
    up, down = packed[:, :128], packed[:, 128:]
    even = parity == 0
    near_ref[...] = jnp.where(even, up, down)
    far_ref[...] = jnp.where(even, down, up)


def ghost_table(near, cross, relay, parity, count):
    rows = near.shape[0]
    first, second = cross[:rows], cross[rows:]
    low = lax.broadcasted_iota(jnp.int32, (rows, 128), 1) < 64
    even = parity == 0
    left = jnp.where(low, jnp.where(even, second, relay), jnp.where(even, first, near))
    right = jnp.where(low, jnp.where(even, near, first), jnp.where(even, relay, second))
    return pieces(unpaired(jnp.concatenate([left, right], axis=1), count))


def send_kernel(parity_ref, state_ref, send_ref, near_ref, far_ref, wide_ref, dense_ref):
    for v in range(NV):
        wide_ref[8 * v : 8 * v + 4, :] = state_ref[v]
        wide_ref[8 * v + 4 : 8 * v + 8, :] = state_ref[v]
    wide = wide_ref[...]
    write_messages(pieces(wide), send_ref[...], parity_ref[0], near_ref, far_ref)
    dense_ref[...] = paired([wide[8 * v : 8 * v + 8] for v in range(NV)])


def gradient_kernel(
    parity_ref, count_ref, wide_ref, near_in, cross_in, relay_in, owner_ref, neighbor_ref, normal_ref,
    volume_ref, send_ref, table_ref, near_ref, far_ref,
):
    parity = parity_ref[0]
    ghosts = ghost_table(near_in[...], cross_in[...], relay_in[...], parity, NV)
    values = jnp.concatenate([pieces(wide_ref[...]), ghosts], axis=1)
    total = jnp.zeros((GROWS, CELLS), F32)
    for f in range(0, FACES, CHUNK):
        own = one_hot(owner_ref[:, f : f + CHUNK], CELLS)
        other = one_hot(neighbor_ref[:, f : f + CHUNK], CELLS + GHOSTS)
        local = other[:CELLS]
        jump_hot = jnp.concatenate([local - own, other[CELLS:]], axis=0).astype(BF)
        sum_hot = (local + own).astype(BF)
        jump = matmul(values, jump_hot)
        jumps = [fold(jump[8 * v : 8 * v + 8]) for v in range(NV)]
        live = lax.broadcasted_iota(jnp.int32, (1, CHUNK), 1) + f < count_ref[0]
        flows = []
        for d in range(3):
            half = jnp.where(live, 0.5 * normal_ref[d : d + 1, f : f + CHUNK], 0.0)
            for v in range(NV):
                flows.append(jumps[v] * half)
        total = total + matmul_t(pieces(jnp.concatenate(flows, axis=0)), sum_hot)
    inverse = 1.0 / volume_ref[...]
    gradient = jnp.concatenate([fold(total[8 * g : 8 * g + 8]) * inverse for g in range(3 * NV)], axis=0)
    table = pieces(gradient)
    table_ref[...] = table
    write_messages(table, send_ref[...], parity, near_ref, far_ref)


def spatial_groups(
    parity_ref, count_ref, wide_ref, near_in, cross_in, relay_in, table_ref, gnear_in, gcross_in, grelay_in,
    owner_ref, neighbor_ref, normal_ref, owner_arm_ref, neighbor_arm_ref, volume_ref,
):
    parity = parity_ref[0]
    ghosts = ghost_table(near_in[...], cross_in[...], relay_in[...], parity, NV)
    grad_ghosts = ghost_table(gnear_in[...], gcross_in[...], grelay_in[...], parity, 3 * NV)
    local = jnp.concatenate([pieces(wide_ref[...]), table_ref[...]], axis=0)
    values = jnp.concatenate([local, jnp.concatenate([ghosts, grad_ghosts], axis=0)], axis=1)
    total = jnp.zeros((VROWS, CELLS), F32)
    top = top_rows((8, CHUNK))
    sign = jnp.where(top, 1.0, -1.0)
    for f in range(0, FACES, CHUNK):
        own = one_hot(owner_ref[:, f : f + CHUNK], CELLS)
        other = one_hot(neighbor_ref[:, f : f + CHUNK], CELLS + GHOSTS)
        difference = (own - other[:CELLS]).astype(BF)
        left = matmul(local, own.astype(BF))
        right = matmul(values, other.astype(BF))
        live = lax.broadcasted_iota(jnp.int32, (1, CHUNK), 1) + f < count_ref[0]
        normals = [jnp.where(live, normal_ref[d : d + 1, f : f + CHUNK], 0.0) for d in range(3)]
        area = jnp.sqrt(normals[0] * normals[0] + normals[1] * normals[1] + normals[2] * normals[2])
        states = []
        for v in range(NV):
            a, b = left[8 * v : 8 * v + 8], right[8 * v : 8 * v + 8]
            for d in range(3):
                g = VROWS + 8 * (NV * d + v)
                a = a + left[g : g + 8] * owner_arm_ref[d : d + 1, f : f + CHUNK]
                b = b + right[g : g + 8] * neighbor_arm_ref[d : d + 1, f : f + CHUNK]
            states.append(jnp.where(top, a, b) + swap_halves(jnp.where(top, b, a)))
        density, energy = states[0], states[4]
        momentum = states[1:4]
        inverse = 1.0 / density
        velocity = [m * inverse for m in momentum]
        kinetic = momentum[0] * velocity[0] + momentum[1] * velocity[1] + momentum[2] * velocity[2]
        pressure = (HEAT_RATIO - 1.0) * (energy - 0.5 * kinetic)
        speed = velocity[0] * normals[0] + velocity[1] * normals[1] + velocity[2] * normals[2]
        wave = jnp.abs(speed) + jnp.sqrt(HEAT_RATIO * pressure * inverse) * area
        wave = jnp.maximum(wave, swap_halves(wave)) * sign
        flux = [density * speed]
        for d in range(3):
            flux.append(momentum[d] * speed + pressure * normals[d])
        flux.append((energy + pressure) * speed)
        faces = [fold(0.5 * (flux[v] + wave * states[v])) for v in range(NV)]
        total = total + matmul_t(pieces(jnp.concatenate(faces, axis=0)), difference)
    inverse = 1.0 / volume_ref[...]
    return [fold(total[8 * v : 8 * v + 8]) * inverse for v in range(NV)]


def middle_kernel(*refs):
    *common, spectral_ref, step_ref, send_ref, wide_out, dense_ref, near_ref, far_ref = refs
    spatial = spatial_groups(*common)
    wide_ref, parity = common[2], common[0][0]
    groups = []
    for v in range(NV):
        rows = slice(8 * v, 8 * v + 8)
        groups.append(wide_ref[rows] - 0.5 * step_ref[...] * (spatial[v] + spectral_ref[rows]))
    wide = jnp.concatenate(groups, axis=0)
    wide_out[...] = wide
    dense_ref[...] = paired(groups)
    write_messages(pieces(wide), send_ref[...], parity, near_ref, far_ref)


def last_kernel(*refs):
    *common, spectral_ref, step_ref, state_ref, new_ref, residual_ref = refs
    spatial = spatial_groups(*common)
    for v in range(NV):
        rate = (spatial[v] + spectral_ref[8 * v : 8 * v + 8])[:4]
        residual_ref[v] = rate
        new_ref[v] = state_ref[v] - step_ref[...] * rate


def spectral_kernel(index_ref, matrix_ref, mine_ref, next_ref, rest_ref, out_ref):
    matrix = matrix_ref[index_ref[0]]
    data = jnp.concatenate([mine_ref[...], next_ref[...], rest_ref[...]], axis=0)
    m_high, d_high = matrix.astype(BF), data.astype(BF)
    m_low, d_low = (matrix - m_high.astype(F32)).astype(BF), (data - d_high.astype(F32)).astype(BF)
    out_ref[...] = matmul(m_high, d_high) + matmul(m_high, d_low) + matmul(m_low, d_high)


def spectral_matrices(groups, size):
    points = groups * size
    distance = np.arange(points)[:, None] - np.arange(points)[None, :]
    safe = np.where(distance == 0, 1, distance)
    table = 0.5 * np.where(distance % 2 == 0, 1.0, -1.0) / np.tan(np.pi * safe / points)
    table = np.where(distance == 0, 0.0, table) * FREQUENCY
    out = np.zeros((groups, VROWS, groups * 24), np.float32)
    for y in range(groups):
        for v in range(NV):
            for s in range(8):
                for b in range(groups):
                    for t in range(size):
                        column = b * 24 + (v // 2) * 8 + (v % 2) * 4 + t
                        out[y, 8 * v + s, column] = table[size * y + s % size, size * (y ^ b) + t]
    return out


def call(kernel, outputs, scalars, arrays, name):
    smem = pl.BlockSpec(memory_space=pltpu.SMEM)
    vmem = pl.BlockSpec(memory_space=pltpu.VMEM)
    return pl.pallas_call(
        kernel,
        out_shape=[jax.ShapeDtypeStruct(s, d) for s, d in outputs],
        in_specs=[smem] * len(scalars) + [vmem] * len(arrays),
        out_specs=[vmem] * len(outputs),
        compiler_params=pltpu.CompilerParams(vmem_limit_bytes=32 << 20),
        name=name,
    )(*scalars, *arrays)


def local(
    state, cell_volume, step_size, face_normal, owner_arm, neighbor_arm, face_owner, face_neighbor, face_count,
    send_cells,
):
    parts = lax.axis_size("dom")
    place = lax.axis_index("dom")
    parity = (place & 1).astype(jnp.int32).reshape(1)
    line = lax.axis_index("inst").astype(jnp.int32).reshape(1)
    volume = cell_volume.reshape(1, CELLS)
    step = step_size.reshape(1, CELLS)
    owner = face_owner.reshape(1, FACES)
    neighbor = face_neighbor.reshape(1, FACES)
    matrices = jnp.asarray(spectral_matrices(lax.axis_size("inst"), state.shape[1]))
    inside = [(i, i ^ 1) for i in range(parts)]
    across = [(i, i + 1) for i in range(1, parts - 1, 2)] + [(i + 1, i) for i in range(1, parts - 1, 2)]

    def exchange(near, far):
        got = lax.ppermute(near, "dom", inside)
        cross = lax.ppermute(jnp.concatenate([far, got], axis=0), "dom", across)
        relay = lax.ppermute(cross[: far.shape[0]], "dom", inside)
        return got, cross, relay

    def instances(dense):
        one = lax.ppermute(dense, "inst", [(i, i ^ 1) for i in range(4)])
        two = lax.ppermute(jnp.concatenate([dense, one], axis=0), "inst", [(i, i ^ 2) for i in range(4)])
        return call(spectral_kernel, [((VROWS, CELLS), F32)], [line], [matrices, dense, one, two], "spectral")[0]

    def message(rows):
        return [((rows, 128), F32)] * 2

    wide_shape, dense_shape = ((VROWS, CELLS), F32), ((24, CELLS), F32)
    geometry = [owner, neighbor, face_normal]
    arms = [owner_arm, neighbor_arm, volume]
    near, far, wide, dense = call(
        send_kernel, message(24) + [wide_shape, dense_shape], [parity], [state, send_cells], "send"
    )
    for section in range(2):
        ghosts = exchange(near, far)
        spectral = instances(dense)
        table, gnear, gfar = call(
            gradient_kernel, [((GROWS, CELLS), BF)] + message(64), [parity, face_count],
            [wide, *ghosts, *geometry, volume, send_cells], "gradient",
        )
        gradient_ghosts = exchange(gnear, gfar)
        common = [wide, *ghosts, table, *gradient_ghosts, *geometry, *arms, spectral, step]
        if section == 0:
            wide, dense, near, far = call(
                middle_kernel, [wide_shape, dense_shape] + message(24), [parity, face_count], [*common, send_cells],
                "middle",
            )
    shape = state.shape
    return tuple(call(last_kernel, [(shape, F32)] * 2, [parity, face_count], [*common, state], "last"))


def solution(mesh):
    placed = (
        P(None, "inst", "dom"), P("dom"), P("dom"), P(None, "dom"), P(None, "dom"), P(None, "dom"), P("dom"), P("dom"),
        P("dom"), P("dom", None),
    )
    return jax.shard_map(
        local, mesh=mesh, in_specs=placed, out_specs=(P(None, "inst", "dom"), P(None, "inst", "dom")), check_vma=False,
    )
```

profile of v0, /device:TPU:129, one launch (start us, length us, event | category | flops | bytes accessed | tf_op | source)
XLA Modules:
  0.0 62.4 jit_solution(7939299980502636648)
XLA Ops:
  0.6 0.7 %copy-done.9 = s32[4,64]{1,0:T(4,128)S(1)} copy-done((s32[4,64]{1,0:T(4,128)S(1)}, s32[4,64]{1,0:T(4,128)}, u32[]{:S(2)}) %copy-start.9) | copy-done | bytes 1048
  1.3 0.8 %copy-done.2 = f32[5,4,512]{2,1,0:T(4,128)S(1)} copy-done((f32[5,4,512]{2,1,0:T(4,128)S(1)}, f32[5,4,512]{2,1,0:T(4,128)}, u32[]{:S(2)}) %copy-start.2) | copy-done | bytes 40984
  2.4 0.8 %collective-permute-start = (f32[24,128]{1,0:T(8,128)S(1)}, f32[24,128]{1,0:T(8,128)S(1)}, u32[]{:S(2)}, u32[]{:S(2)}) collective-permute-start(f32[24,128]{1,0:T(8,128)S(1)} %get-tuple-element.17), channel_id=1, source_target_pairs={{0,4},{4,0},{8,12},{12,8},{16,20},{20,16},{24,28},{28,24},{32,36},... | collective-permute-start | bytes 36872 | tf_op jit(solution)/shard_map/ppermute | solution.py:262
  3.1 1.3 %collective-permute-start.6 = (f32[24,512]{1,0:T(8,128)S(1)}, f32[24,512]{1,0:T(8,128)S(1)}, u32[]{:S(2)}, u32[]{:S(2)}) collective-permute-start(f32[24,512]{1,0:T(8,128)S(1)} %get-tuple-element.22.mine_ref), channel_id=1, source_target_pairs={{0,1},{1,0},{2,3},{3,2},{4,5},{5,4},{6,7},{7,6},{8,9},{9,8},{10,11... | collective-permute-start | bytes 147464 | tf_op jit(solution)/shard_map/ppermute | solution.py:268
  4.5 3.4 %collective-permute-start.1 = (f32[48,128]{1,0:T(8,128)S(1)}, f32[48,128]{1,0:T(8,128)S(1)}, u32[]{:S(2)}, u32[]{:S(2)}) collective-permute-start(f32[48,128]{1,0:T(8,128)S(1)} %pad_maximum_fusion.4), channel_id=1, source_target_pairs={{4,8},{12,16},{20,24},{28,32},{36,40},{44,48},{52,56},{60,64},{68,... | collective-permute-start | bytes 73736 | tf_op jit(solution)/shard_map/ppermute | solution.py:263
  7.8 1.8 %collective-permute-done.1.cross_in.refs_4_ = f32[48,128]{1,0:T(8,128)S(1)} collective-permute-done((f32[48,128]{1,0:T(8,128)S(1)}, f32[48,128]{1,0:T(8,128)S(1)}, u32[]{:S(2)}, u32[]{:S(2)}) %collective-permute-start.1) | collective-permute-done | bytes 24608 | tf_op jit(solution)/shard_map/ppermute | solution.py:263
  9.6 3.8 %collective-permute-start.2 = (f32[24,128]{1,0:T(8,128)S(1)}, f32[24,128]{1,0:T(8,128)S(1)}, u32[]{:S(2)}, u32[]{:S(2)}) collective-permute-start(f32[24,128]{1,0:T(8,128)S(1)} %slice.16), channel_id=1, source_target_pairs={{0,4},{4,0},{8,12},{12,8},{16,20},{20,16},{24,28},{28,24},{32,36},... | collective-permute-start | bytes 36872 | tf_op jit(solution)/shard_map/ppermute | solution.py:264
  14.3 2.4 %gradient.2 = (bf16[120,512]{1,0:T(8,128)(2,1)S(1)}, f32[64,128]{1,0:T(8,128)S(1)}, f32[64,128]{1,0:T(8,128)S(1)}) custom-call(s32[1]{0:T(128)} %bitcast.parity_ref.refs_0_, s32[1]{0:T(128)S(6)} %copy.13.count_ref.refs_1_, f32[40,512]{1,0:T(8,128)S(1)} %get-tuple-element.16.wide_ref.refs_2_, f32[24,128]{1,0:T(8,128)S(1)} %collective-permute-done.near_in.refs_3_, ...), custom_call_target="tpu_custom_call" | custom-call | tf_op jit(solution)/shard_map/gradient/pallas_call | solution.py:235
  17.1 2.7 %collective-permute-start.7 = (f32[48,512]{1,0:T(8,128)S(1)}, f32[48,512]{1,0:T(8,128)S(1)}, u32[]{:S(2)}, u32[]{:S(2)}) collective-permute-start(f32[48,512]{1,0:T(8,128)S(1)} %pad_maximum_fusion), channel_id=1, source_target_pairs={{0,2},{1,3},{2,0},{3,1},{4,6},{5,7},{6,4},{7,5},{8,10},{9,11},{10,... | collective-permute-start | bytes 294920 | tf_op jit(solution)/shard_map/ppermute | solution.py:269
  19.8 2.1 %collective-permute-start.4 = (f32[128,128]{1,0:T(8,128)S(1)}, f32[128,128]{1,0:T(8,128)S(1)}, u32[]{:S(2)}, u32[]{:S(2)}) collective-permute-start(f32[128,128]{1,0:T(8,128)S(1)} %pad_maximum_fusion.2), channel_id=1, source_target_pairs={{4,8},{12,16},{20,24},{28,32},{36,40},{44,48},{52,56},{60,64},{68,... | collective-permute-start | bytes 196616 | tf_op jit(solution)/shard_map/ppermute | solution.py:263
  21.8 3.7 %collective-permute-done.4.refs_8_ = f32[128,128]{1,0:T(8,128)S(1)} collective-permute-done((f32[128,128]{1,0:T(8,128)S(1)}, f32[128,128]{1,0:T(8,128)S(1)}, u32[]{:S(2)}, u32[]{:S(2)}) %collective-permute-start.4) | collective-permute-done | bytes 65568 | tf_op jit(solution)/shard_map/ppermute | solution.py:263
  25.5 3.8 %collective-permute-start.5 = (f32[64,128]{1,0:T(8,128)S(1)}, f32[64,128]{1,0:T(8,128)S(1)}, u32[]{:S(2)}, u32[]{:S(2)}) collective-permute-start(f32[64,128]{1,0:T(8,128)S(1)} %slice.17), channel_id=1, source_target_pairs={{0,4},{4,0},{8,12},{12,8},{16,20},{20,16},{24,28},{28,24},{32,36},... | collective-permute-start | bytes 98312 | tf_op jit(solution)/shard_map/ppermute | solution.py:264
  30.2 3.3 %middle.1 = (f32[40,512]{1,0:T(8,128)S(1)}, f32[24,512]{1,0:T(8,128)S(1)}, f32[24,128]{1,0:T(8,128)S(1)}, f32[24,128]{1,0:T(8,128)S(1)}) custom-call(s32[1]{0:T(128)} %bitcast.parity_ref.refs_0_, s32[1]{0:T(128)S(6)} %copy.13.count_ref.refs_1_, f32[40,512]{1,0:T(8,128)S(1)} %get-tuple-element.16.wide_ref.refs_2_, ...), custom_call_target="tpu_custom_call" | custom-call | tf_op jit(solution)/shard_map/middle/pallas_call | solution.py:235
  34.7 1.9 %collective-permute-start.9 = (f32[48,128]{1,0:T(8,128)S(1)}, f32[48,128]{1,0:T(8,128)S(1)}, u32[]{:S(2)}, u32[]{:S(2)}) collective-permute-start(f32[48,128]{1,0:T(8,128)S(1)} %pad_maximum_fusion.5), channel_id=1, source_target_pairs={{4,8},{12,16},{20,24},{28,32},{36,40},{44,48},{52,56},{60,64},{68,... | collective-permute-start | bytes 73736 | tf_op jit(solution)/shard_map/ppermute | solution.py:263
  36.6 3.2 %collective-permute-done.9.cross_in.refs_4_ = f32[48,128]{1,0:T(8,128)S(1)} collective-permute-done((f32[48,128]{1,0:T(8,128)S(1)}, f32[48,128]{1,0:T(8,128)S(1)}, u32[]{:S(2)}, u32[]{:S(2)}) %collective-permute-start.9) | collective-permute-done | bytes 24608 | tf_op jit(solution)/shard_map/ppermute | solution.py:263
  39.9 3.6 %collective-permute-start.10 = (f32[24,128]{1,0:T(8,128)S(1)}, f32[24,128]{1,0:T(8,128)S(1)}, u32[]{:S(2)}, u32[]{:S(2)}) collective-permute-start(f32[24,128]{1,0:T(8,128)S(1)} %slice.18), channel_id=1, source_target_pairs={{0,4},{4,0},{8,12},{12,8},{16,20},{20,16},{24,28},{28,24},{32,36},... | collective-permute-start | bytes 36872 | tf_op jit(solution)/shard_map/ppermute | solution.py:264
  43.5 0.8 %collective-permute-done.10.relay_in.refs_5_ = f32[24,128]{1,0:T(8,128)S(1)} collective-permute-done((f32[24,128]{1,0:T(8,128)S(1)}, f32[24,128]{1,0:T(8,128)S(1)}, u32[]{:S(2)}, u32[]{:S(2)}) %collective-permute-start.10) | collective-permute-done | bytes 12320 | tf_op jit(solution)/shard_map/ppermute | solution.py:264
  44.3 2.3 %gradient.3 = (bf16[120,512]{1,0:T(8,128)(2,1)S(1)}, f32[64,128]{1,0:T(8,128)S(1)}, f32[64,128]{1,0:T(8,128)S(1)}) custom-call(s32[1]{0:T(128)} %bitcast.parity_ref.refs_0_, s32[1]{0:T(128)S(6)} %copy.13.count_ref.refs_1_, f32[40,512]{1,0:T(8,128)S(1)} %get-tuple-element.23.wide_ref.refs_2_, f32[24,128]{1,0:T(8,128)S(1)} %collective-permute-done.8.near_in.refs_3_, ...), custom_call_target="tpu_custom_call" | custom-call | tf_op jit(solution)/shard_map/gradient/pallas_call | solution.py:235
  47.1 1.2 %collective-permute-start.15 = (f32[48,512]{1,0:T(8,128)S(1)}, f32[48,512]{1,0:T(8,128)S(1)}, u32[]{:S(2)}, u32[]{:S(2)}) collective-permute-start(f32[48,512]{1,0:T(8,128)S(1)} %pad_maximum_fusion.1), channel_id=1, source_target_pairs={{0,2},{1,3},{2,0},{3,1},{4,6},{5,7},{6,4},{7,5},{8,10},{9,11},{10,... | collective-permute-start | bytes 294920 | tf_op jit(solution)/shard_map/ppermute | solution.py:269
  48.4 1.9 %collective-permute-start.12 = (f32[128,128]{1,0:T(8,128)S(1)}, f32[128,128]{1,0:T(8,128)S(1)}, u32[]{:S(2)}, u32[]{:S(2)}) collective-permute-start(f32[128,128]{1,0:T(8,128)S(1)} %pad_maximum_fusion.3), channel_id=1, source_target_pairs={{4,8},{12,16},{20,24},{28,32},{36,40},{44,48},{52,56},{60,64},{68,... | collective-permute-start | bytes 196616 | tf_op jit(solution)/shard_map/ppermute | solution.py:263
  50.3 3.7 %collective-permute-done.12.refs_8_ = f32[128,128]{1,0:T(8,128)S(1)} collective-permute-done((f32[128,128]{1,0:T(8,128)S(1)}, f32[128,128]{1,0:T(8,128)S(1)}, u32[]{:S(2)}, u32[]{:S(2)}) %collective-permute-start.12) | collective-permute-done | bytes 65568 | tf_op jit(solution)/shard_map/ppermute | solution.py:263
  54.0 3.8 %collective-permute-start.13 = (f32[64,128]{1,0:T(8,128)S(1)}, f32[64,128]{1,0:T(8,128)S(1)}, u32[]{:S(2)}, u32[]{:S(2)}) collective-permute-start(f32[64,128]{1,0:T(8,128)S(1)} %slice.19), channel_id=1, source_target_pairs={{0,4},{4,0},{8,12},{12,8},{16,20},{20,16},{24,28},{28,24},{32,36},... | collective-permute-start | bytes 98312 | tf_op jit(solution)/shard_map/ppermute | solution.py:264
  57.9 0.7 %collective-permute-done.13.refs_9_ = f32[64,128]{1,0:T(8,128)S(1)} collective-permute-done((f32[64,128]{1,0:T(8,128)S(1)}, f32[64,128]{1,0:T(8,128)S(1)}, u32[]{:S(2)}, u32[]{:S(2)}) %collective-permute-start.13) | collective-permute-done | bytes 32800 | tf_op jit(solution)/shard_map/ppermute | solution.py:264
  58.6 3.8 %last.1 = (f32[5,4,512]{2,1,0:T(4,128)}, f32[5,4,512]{2,1,0:T(4,128)}) custom-call(s32[1]{0:T(128)} %bitcast.parity_ref.refs_0_, s32[1]{0:T(128)S(6)} %copy.13.count_ref.refs_1_, f32[40,512]{1,0:T(8,128)S(1)} %get-tuple-element.23.wide_ref.refs_2_, f32[24,128]{1,0:T(8,128)S(1)} %collective-permute-done.8.near_in.refs_3_, ...), custom_call_target="tpu_custom_call" | custom-call | tf_op jit(solution)/shard_map/last/pallas_call | solution.py:235
  (47 shorter events, 3.7 us)
Async XLA Ops:
  2.4 2.1 %collective-permute-start = (f32[24,128]{1,0:T(8,128)S(1)}, f32[24,128]{1,0:T(8,128)S(1)}, u32[]{:S(2)}, u32[]{:S(2)}) collective-permute-start(f32[24,128]{1,0:T(8,128)S(1)} %get-tuple-element.17), channel_id=1, source_target_pairs={{0,4},{4,0},{8,12},{12,8},{16,20},{20,16},{24,28},{28,24},{32,36},... | collective-permute-start | bytes 36872 | tf_op jit(solution)/shard_map/ppermute | solution.py:262
  3.1 13.9 %collective-permute-start.6 = (f32[24,512]{1,0:T(8,128)S(1)}, f32[24,512]{1,0:T(8,128)S(1)}, u32[]{:S(2)}, u32[]{:S(2)}) collective-permute-start(f32[24,512]{1,0:T(8,128)S(1)} %get-tuple-element.22.mine_ref), channel_id=1, source_target_pairs={{0,1},{1,0},{2,3},{3,2},{4,5},{5,4},{6,7},{7,6},{8,9},{9,8},{10,11... | collective-permute-start | bytes 147464 | tf_op jit(solution)/shard_map/ppermute | solution.py:268
  4.4 9.8 %copy-start = (f32[3,2048]{1,0:T(4,128)S(1)}, f32[3,2048]{1,0:T(4,128)}, u32[]{:S(2)}) copy-start(f32[3,2048]{1,0:T(4,128)} %refs_12_.3) | copy-start | bytes 73732
  4.5 5.1 %collective-permute-start.1 = (f32[48,128]{1,0:T(8,128)S(1)}, f32[48,128]{1,0:T(8,128)S(1)}, u32[]{:S(2)}, u32[]{:S(2)}) collective-permute-start(f32[48,128]{1,0:T(8,128)S(1)} %pad_maximum_fusion.4), channel_id=1, source_target_pairs={{4,8},{12,16},{20,24},{28,32},{36,40},{44,48},{52,56},{60,64},{68,... | collective-permute-start | bytes 73736 | tf_op jit(solution)/shard_map/ppermute | solution.py:263
  9.6 4.6 %copy-start.5 = (s32[2048]{0:T(1024)S(1)}, s32[2048]{0:T(1024)}, u32[]{:S(2)}) copy-start(s32[2048]{0:T(1024)} %param.18) | copy-start | bytes 24580
  9.6 4.6 %copy-start.8 = (f32[512]{0:T(512)S(1)}, f32[512]{0:T(512)}, u32[]{:S(2)}) copy-start(f32[512]{0:T(512)} %param.12) | copy-start | bytes 6148
  9.6 4.6 %copy-start.4 = (s32[2048]{0:T(1024)S(1)}, s32[2048]{0:T(1024)}, u32[]{:S(2)}) copy-start(s32[2048]{0:T(1024)} %param.17) | copy-start | bytes 24580
  9.6 4.6 %collective-permute-start.2 = (f32[24,128]{1,0:T(8,128)S(1)}, f32[24,128]{1,0:T(8,128)S(1)}, u32[]{:S(2)}, u32[]{:S(2)}) collective-permute-start(f32[24,128]{1,0:T(8,128)S(1)} %slice.16), channel_id=1, source_target_pairs={{0,4},{4,0},{8,12},{12,8},{16,20},{20,16},{24,28},{28,24},{32,36},... | collective-permute-start | bytes 36872 | tf_op jit(solution)/shard_map/ppermute | solution.py:264
  16.6 3.2 %collective-permute-start.3 = (f32[64,128]{1,0:T(8,128)S(1)}, f32[64,128]{1,0:T(8,128)S(1)}, u32[]{:S(2)}, u32[]{:S(2)}) collective-permute-start(f32[64,128]{1,0:T(8,128)S(1)} %get-tuple-element.20), channel_id=1, source_target_pairs={{0,4},{4,0},{8,12},{12,8},{16,20},{20,16},{24,28},{28,24},{32,36},... | collective-permute-start | bytes 98312 | tf_op jit(solution)/shard_map/ppermute | solution.py:262
  17.1 12.2 %collective-permute-start.7 = (f32[48,512]{1,0:T(8,128)S(1)}, f32[48,512]{1,0:T(8,128)S(1)}, u32[]{:S(2)}, u32[]{:S(2)}) collective-permute-start(f32[48,512]{1,0:T(8,128)S(1)} %pad_maximum_fusion), channel_id=1, source_target_pairs={{0,2},{1,3},{2,0},{3,1},{4,6},{5,7},{6,4},{7,5},{8,10},{9,11},{10,... | collective-permute-start | bytes 294920 | tf_op jit(solution)/shard_map/ppermute | solution.py:269
  19.8 9.5 %copy-start.1 = (f32[4,40,96]{2,1,0:T(8,128)S(1)}, f32[4,40,96]{2,1,0:T(8,128)}, u32[]{:S(2)}) copy-start(f32[4,40,96]{2,1,0:T(8,128)} %constant.13.clone.matrix_ref) | copy-start | bytes 184324
  19.8 5.7 %collective-permute-start.4 = (f32[128,128]{1,0:T(8,128)S(1)}, f32[128,128]{1,0:T(8,128)S(1)}, u32[]{:S(2)}, u32[]{:S(2)}) collective-permute-start(f32[128,128]{1,0:T(8,128)S(1)} %pad_maximum_fusion.2), channel_id=1, source_target_pairs={{4,8},{12,16},{20,24},{28,32},{36,40},{44,48},{52,56},{60,64},{68,... | collective-permute-start | bytes 196616 | tf_op jit(solution)/shard_map/ppermute | solution.py:263
  25.5 4.6 %collective-permute-start.5 = (f32[64,128]{1,0:T(8,128)S(1)}, f32[64,128]{1,0:T(8,128)S(1)}, u32[]{:S(2)}, u32[]{:S(2)}) collective-permute-start(f32[64,128]{1,0:T(8,128)S(1)} %slice.17), channel_id=1, source_target_pairs={{0,4},{4,0},{8,12},{12,8},{16,20},{20,16},{24,28},{28,24},{32,36},... | collective-permute-start | bytes 98312 | tf_op jit(solution)/shard_map/ppermute | solution.py:264
  29.3 0.9 %copy-start.6 = (f32[3,2048]{1,0:T(4,128)S(1)}, f32[3,2048]{1,0:T(4,128)}, u32[]{:S(2)}) copy-start(f32[3,2048]{1,0:T(4,128)} %refs_13_.3) | copy-start | bytes 73732
  29.3 0.9 %copy-start.7 = (f32[3,2048]{1,0:T(4,128)S(1)}, f32[3,2048]{1,0:T(4,128)}, u32[]{:S(2)}) copy-start(f32[3,2048]{1,0:T(4,128)} %refs_14_.3) | copy-start | bytes 73732
  33.5 1.3 %collective-permute-start.8 = (f32[24,128]{1,0:T(8,128)S(1)}, f32[24,128]{1,0:T(8,128)S(1)}, u32[]{:S(2)}, u32[]{:S(2)}) collective-permute-start(f32[24,128]{1,0:T(8,128)S(1)} %get-tuple-element.24), channel_id=1, source_target_pairs={{0,4},{4,0},{8,12},{12,8},{16,20},{20,16},{24,28},{28,24},{32,36},... | collective-permute-start | bytes 36872 | tf_op jit(solution)/shard_map/ppermute | solution.py:262
  33.9 13.3 %collective-permute-start.14 = (f32[24,512]{1,0:T(8,128)S(1)}, f32[24,512]{1,0:T(8,128)S(1)}, u32[]{:S(2)}, u32[]{:S(2)}) collective-permute-start(f32[24,512]{1,0:T(8,128)S(1)} %get-tuple-element.29.mine_ref), channel_id=1, source_target_pairs={{0,1},{1,0},{2,3},{3,2},{4,5},{5,4},{6,7},{7,6},{8,9},{9,8},{10,11... | collective-permute-start | bytes 147464 | tf_op jit(solution)/shard_map/ppermute | solution.py:268
  34.7 5.1 %collective-permute-start.9 = (f32[48,128]{1,0:T(8,128)S(1)}, f32[48,128]{1,0:T(8,128)S(1)}, u32[]{:S(2)}, u32[]{:S(2)}) collective-permute-start(f32[48,128]{1,0:T(8,128)S(1)} %pad_maximum_fusion.5), channel_id=1, source_target_pairs={{4,8},{12,16},{20,24},{28,32},{36,40},{44,48},{52,56},{60,64},{68,... | collective-permute-start | bytes 73736 | tf_op jit(solution)/shard_map/ppermute | solution.py:263
  39.9 4.5 %collective-permute-start.10 = (f32[24,128]{1,0:T(8,128)S(1)}, f32[24,128]{1,0:T(8,128)S(1)}, u32[]{:S(2)}, u32[]{:S(2)}) collective-permute-start(f32[24,128]{1,0:T(8,128)S(1)} %slice.18), channel_id=1, source_target_pairs={{0,4},{4,0},{8,12},{12,8},{16,20},{20,16},{24,28},{28,24},{32,36},... | collective-permute-start | bytes 36872 | tf_op jit(solution)/shard_map/ppermute | solution.py:264
  46.7 1.7 %collective-permute-start.11 = (f32[64,128]{1,0:T(8,128)S(1)}, f32[64,128]{1,0:T(8,128)S(1)}, u32[]{:S(2)}, u32[]{:S(2)}) collective-permute-start(f32[64,128]{1,0:T(8,128)S(1)} %get-tuple-element.27), channel_id=1, source_target_pairs={{0,4},{4,0},{8,12},{12,8},{16,20},{20,16},{24,28},{28,24},{32,36},... | collective-permute-start | bytes 98312 | tf_op jit(solution)/shard_map/ppermute | solution.py:262
  47.1 10.6 %collective-permute-start.15 = (f32[48,512]{1,0:T(8,128)S(1)}, f32[48,512]{1,0:T(8,128)S(1)}, u32[]{:S(2)}, u32[]{:S(2)}) collective-permute-start(f32[48,512]{1,0:T(8,128)S(1)} %pad_maximum_fusion.1), channel_id=1, source_target_pairs={{0,2},{1,3},{2,0},{3,1},{4,6},{5,7},{6,4},{7,5},{8,10},{9,11},{10,... | collective-permute-start | bytes 294920 | tf_op jit(solution)/shard_map/ppermute | solution.py:269
  48.4 5.6 %collective-permute-start.12 = (f32[128,128]{1,0:T(8,128)S(1)}, f32[128,128]{1,0:T(8,128)S(1)}, u32[]{:S(2)}, u32[]{:S(2)}) collective-permute-start(f32[128,128]{1,0:T(8,128)S(1)} %pad_maximum_fusion.3), channel_id=1, source_target_pairs={{4,8},{12,16},{20,24},{28,32},{36,40},{44,48},{52,56},{60,64},{68,... | collective-permute-start | bytes 196616 | tf_op jit(solution)/shard_map/ppermute | solution.py:263
  54.0 4.6 %copy-start.3 = (f32[5,4,512]{2,1,0:T(4,128)S(1)}, f32[5,4,512]{2,1,0:T(4,128)}, u32[]{:S(2)}) copy-start(f32[5,4,512]{2,1,0:T(4,128)} %refs_18_.3) | copy-start | bytes 122884
  54.0 4.6 %collective-permute-start.13 = (f32[64,128]{1,0:T(8,128)S(1)}, f32[64,128]{1,0:T(8,128)S(1)}, u32[]{:S(2)}, u32[]{:S(2)}) collective-permute-start(f32[64,128]{1,0:T(8,128)S(1)} %slice.19), channel_id=1, source_target_pairs={{0,4},{4,0},{8,12},{12,8},{16,20},{20,16},{24,28},{28,24},{32,36},... | collective-permute-start | bytes 98312 | tf_op jit(solution)/shard_map/ppermute | solution.py:264
  (3 other events, 2.2 us)
where the time goes:
time: 62.8 us; the launch traced here: 62.4 us
  starting transfers between devices  31.8 us (51%)
  waiting for transfers between devices  15.2 us (24%)
  Pallas kernels  12.4 us (20%)
  local copies, waits for them, and re-layouts  1.53 us (2%)
  between operations  1.42 us (2%)
    ppermute x4, starting transfers between devices, exchange(): relay = lax.ppermute(cross[:far.shape[0]], 'dom', inside)  15 us
    pallas_call x7, Pallas kernels, call(): pl.pallas_call(kernel, out_shape=[jax.ShapeDtypeStruct(s, d) for s, d in...  12.4 us
    ppermute x4, waiting for transfers between devices, exchange(): cross = lax.ppermute(jnp.concatenate([far, got], axis=0), 'dom', across)  12.3 us
    ppermute x4, starting transfers between devices, exchange(): cross = lax.ppermute(jnp.concatenate([far, got], axis=0), 'dom', across)  9.27 us
    ppermute x2, starting transfers between devices, instances(): lax.ppermute(jnp.concatenate([dense, one], axis=0), 'inst', [(i, i ^ 2) f...  3.94 us
    ppermute x4, waiting for transfers between devices, exchange(): relay = lax.ppermute(cross[:far.shape[0]], 'dom', inside)  2.35 us
    ppermute x4, starting transfers between devices, exchange(): got = lax.ppermute(near, 'dom', inside)  2.05 us
    ppermute x2, starting transfers between devices, instances(): one = lax.ppermute(dense, 'inst', [(i, i ^ 1) for i in range(4)])  1.6 us
  transfers between devices with their start and end apart: 16, of which 9 were waited for; matrix products, arithmetic and copies ran while one was open for 0% of the time, Pallas kernels for 8%

commit v1 on v0

--- a/solution.py
+++ b/solution.py
@@ -1,5 +1,3 @@
-import functools
-
 import jax
 import jax.numpy as jnp
 import numpy as np
@@ -7,6 +5,7 @@
 from jax.experimental import pallas as pl
 from jax.experimental.pallas import tpu as pltpu
 from jax.sharding import PartitionSpec as P
+
 
 HEAT_RATIO = 1.4
 FREQUENCY = 0.5
@@ -225,11 +224,11 @@
                 for b in range(groups):
                     for t in range(size):
                         column = b * 24 + (v // 2) * 8 + (v % 2) * 4 + t
-                        out[y, 8 * v + s, column] = table[size * y + s % size, size * (y ^ b) + t]
+                        out[y, 8 * v + s, column] = table[size * y + s % size, size * (y ^ (0, 2, 1, 3)[b]) + t]
     return out
 
 
-def call(kernel, outputs, scalars, arrays, name):
+def call(kernel, outputs, scalars, arrays):
     smem = pl.BlockSpec(memory_space=pltpu.SMEM)
     vmem = pl.BlockSpec(memory_space=pltpu.VMEM)
     return pl.pallas_call(
@@ -238,7 +237,6 @@
         in_specs=[smem] * len(scalars) + [vmem] * len(arrays),
         out_specs=[vmem] * len(outputs),
         compiler_params=pltpu.CompilerParams(vmem_limit_bytes=32 << 20),
-        name=name,
     )(*scalars, *arrays)
 
 
@@ -256,18 +254,20 @@
     neighbor = face_neighbor.reshape(1, FACES)
     matrices = jnp.asarray(spectral_matrices(lax.axis_size("inst"), state.shape[1]))
     inside = [(i, i ^ 1) for i in range(parts)]
-    across = [(i, i + 1) for i in range(1, parts - 1, 2)] + [(i + 1, i) for i in range(1, parts - 1, 2)]
+    across = [(i, (i + 1) % parts) for i in range(1, parts, 2)] + [((i + 1) % parts, i) for i in range(1, parts, 2)]
 
     def exchange(near, far):
         got = lax.ppermute(near, "dom", inside)
-        cross = lax.ppermute(jnp.concatenate([far, got], axis=0), "dom", across)
+        outgoing = jnp.concatenate([far, got], axis=0)
+        cross = lax.ppermute(outgoing, "dom", across)
         relay = lax.ppermute(cross[: far.shape[0]], "dom", inside)
         return got, cross, relay
 
     def instances(dense):
-        one = lax.ppermute(dense, "inst", [(i, i ^ 1) for i in range(4)])
-        two = lax.ppermute(jnp.concatenate([dense, one], axis=0), "inst", [(i, i ^ 2) for i in range(4)])
-        return call(spectral_kernel, [((VROWS, CELLS), F32)], [line], [matrices, dense, one, two], "spectral")[0]
+        one = lax.ppermute(dense, "inst", [(i, i ^ 2) for i in range(4)])
+        outgoing = jnp.concatenate([dense, one], axis=0)
+        two = lax.ppermute(outgoing, "inst", [(i, i ^ 1) for i in range(4)])
+        return call(spectral_kernel, [((VROWS, CELLS), F32)], [line], [matrices, dense, one, two])[0]
 
     def message(rows):
         return [((rows, 128), F32)] * 2
@@ -275,25 +275,22 @@
     wide_shape, dense_shape = ((VROWS, CELLS), F32), ((24, CELLS), F32)
     geometry = [owner, neighbor, face_normal]
     arms = [owner_arm, neighbor_arm, volume]
-    near, far, wide, dense = call(
-        send_kernel, message(24) + [wide_shape, dense_shape], [parity], [state, send_cells], "send"
-    )
+    near, far, wide, dense = call(send_kernel, message(24) + [wide_shape, dense_shape], [parity], [state, send_cells])
     for section in range(2):
         ghosts = exchange(near, far)
         spectral = instances(dense)
         table, gnear, gfar = call(
             gradient_kernel, [((GROWS, CELLS), BF)] + message(64), [parity, face_count],
-            [wide, *ghosts, *geometry, volume, send_cells], "gradient",
+            [wide, *ghosts, *geometry, volume, send_cells],
         )
         gradient_ghosts = exchange(gnear, gfar)
         common = [wide, *ghosts, table, *gradient_ghosts, *geometry, *arms, spectral, step]
         if section == 0:
             wide, dense, near, far = call(
                 middle_kernel, [wide_shape, dense_shape] + message(24), [parity, face_count], [*common, send_cells],
-                "middle",
             )
     shape = state.shape
-    return tuple(call(last_kernel, [(shape, F32)] * 2, [parity, face_count], [*common, state], "last"))
+    return tuple(call(last_kernel, [(shape, F32)] * 2, [parity, face_count], [*common, state]))
 
 
 def solution(mesh):

time: 62.8 us -> 58.4 us (0.930)
  the two profiles are of different devices: /device:TPU:129 before, /device:TPU:1 now
where the time goes in v1:
time: 58.4 us; the launch traced here: 58.1 us
  starting transfers between devices  26 us (45%)
  waiting for transfers between devices  16.8 us (29%)
  Pallas kernels  12.4 us (21%)
  local copies, waits for them, and re-layouts  1.53 us (3%)
  between operations  1.41 us (2%)
    ppermute x4, starting transfers between devices, exchange(): relay = lax.ppermute(cross[:far.shape[0]], 'dom', inside)  16.5 us
    ppermute x4, waiting for transfers between devices, exchange(): cross = lax.ppermute(outgoing, 'dom', across)  13.5 us
    pallas_call x7, Pallas kernels, call(): pl.pallas_call(kernel, out_shape=[jax.ShapeDtypeStruct(s, d) for s, d in...  12.4 us
    ppermute x4, starting transfers between devices, exchange(): got = lax.ppermute(near, 'dom', inside)  4.57 us
    ppermute x2, starting transfers between devices, instances(): one = lax.ppermute(dense, 'inst', [(i, i ^ 2) for i in range(4)])  2.5 us
    ppermute x4, waiting for transfers between devices, exchange(): relay = lax.ppermute(cross[:far.shape[0]], 'dom', inside)  2.35 us
    ppermute x4, starting transfers between devices, exchange(): cross = lax.ppermute(outgoing, 'dom', across)  1.66 us
    unnamed x22, local copies, waits for them, and re-layouts  1.52 us
  transfers between devices with their start and end apart: 16, of which 10 were waited for; matrix products, arithmetic and copies ran while one was open for 0% of the time, Pallas kernels for 9%

profile of v1, /device:TPU:1, one launch (start us, length us, event | category | flops | bytes accessed | tf_op | source)
XLA Modules:
  0.0 58.1 jit_solution(14817230396050300789)
XLA Ops:
  0.6 0.7 %copy-done.9 = s32[4,64]{1,0:T(4,128)S(1)} copy-done((s32[4,64]{1,0:T(4,128)S(1)}, s32[4,64]{1,0:T(4,128)}, u32[]{:S(2)}) %copy-start.9) | copy-done | bytes 1048
  1.3 0.8 %copy-done.2 = f32[5,4,512]{2,1,0:T(4,128)S(1)} copy-done((f32[5,4,512]{2,1,0:T(4,128)S(1)}, f32[5,4,512]{2,1,0:T(4,128)}, u32[]{:S(2)}) %copy-start.2) | copy-done | bytes 40984
  2.4 3.3 %collective-permute-start = (f32[24,128]{1,0:T(8,128)S(1)}, f32[24,128]{1,0:T(8,128)S(1)}, u32[]{:S(2)}, u32[]{:S(2)}) collective-permute-start(f32[24,128]{1,0:T(8,128)S(1)} %get-tuple-element.17), channel_id=1, source_target_pairs={{0,4},{4,0},{8,12},{12,8},{16,20},{20,16},{24,28},{28,24},{32,36},... | collective-permute-start | bytes 36872 | tf_op jit(solution)/shard_map/ppermute | solution.py:260
  5.7 1.2 %collective-permute-start.6 = (f32[24,512]{1,0:T(8,128)S(1)}, f32[24,512]{1,0:T(8,128)S(1)}, u32[]{:S(2)}, u32[]{:S(2)}) collective-permute-start(f32[24,512]{1,0:T(8,128)S(1)} %get-tuple-element.22.mine_ref), channel_id=1, source_target_pairs={{0,2},{1,3},{2,0},{3,1},{4,6},{5,7},{6,4},{7,5},{8,10},{9,11},{10,... | collective-permute-start | bytes 147464 | tf_op jit(solution)/shard_map/ppermute | solution.py:267
  6.9 1.6 %collective-permute-start.1 = (f32[48,128]{1,0:T(8,128)S(1)}, f32[48,128]{1,0:T(8,128)S(1)}, u32[]{:S(2)}, u32[]{:S(2)}) collective-permute-start(f32[48,128]{1,0:T(8,128)S(1)} %pad_maximum_fusion.4), channel_id=1, source_target_pairs={{4,8},{12,16},{20,24},{28,32},{36,40},{44,48},{52,56},{60,64},{68,... | collective-permute-start | bytes 73736 | tf_op jit(solution)/shard_map/ppermute | solution.py:262
  8.5 2.1 %collective-permute-done.1.cross_in.refs_4_ = f32[48,128]{1,0:T(8,128)S(1)} collective-permute-done((f32[48,128]{1,0:T(8,128)S(1)}, f32[48,128]{1,0:T(8,128)S(1)}, u32[]{:S(2)}, u32[]{:S(2)}) %collective-permute-start.1) | collective-permute-done | bytes 24608 | tf_op jit(solution)/shard_map/ppermute | solution.py:262
  10.5 6.2 %collective-permute-start.2 = (f32[24,128]{1,0:T(8,128)S(1)}, f32[24,128]{1,0:T(8,128)S(1)}, u32[]{:S(2)}, u32[]{:S(2)}) collective-permute-start(f32[24,128]{1,0:T(8,128)S(1)} %slice.16), channel_id=1, source_target_pairs={{0,4},{4,0},{8,12},{12,8},{16,20},{20,16},{24,28},{28,24},{32,36},... | collective-permute-start | bytes 36872 | tf_op jit(solution)/shard_map/ppermute | solution.py:263
  17.6 2.4 %shard_map.123 = (bf16[120,512]{1,0:T(8,128)(2,1)S(1)}, f32[64,128]{1,0:T(8,128)S(1)}, f32[64,128]{1,0:T(8,128)S(1)}) custom-call(s32[1]{0:T(128)} %bitcast.parity_ref.refs_0_, s32[1]{0:T(128)S(6)} %copy.13.count_ref.refs_1_, f32[40,512]{1,0:T(8,128)S(1)} %get-tuple-element.16.wide_ref.refs_2_, f32[24,128]{1,0:T(8,128)S(1)} %collective-permute-done.near_in.refs_3_, ...), custom_call_target="tpu_custom_call" | custom-call | tf_op jit(solution)/shard_map/pallas_call | solution.py:234
  20.0 0.4 collective-permute-start.3
  20.4 0.5 collective-permute-start.7
  21.4 4.0 %collective-permute-done.4.refs_8_ = f32[128,128]{1,0:T(8,128)S(1)} collective-permute-done((f32[128,128]{1,0:T(8,128)S(1)}, f32[128,128]{1,0:T(8,128)S(1)}, u32[]{:S(2)}, u32[]{:S(2)}) %collective-permute-start.4) | collective-permute-done | bytes 65568 | tf_op jit(solution)/shard_map/ppermute | solution.py:262
  25.3 3.4 %collective-permute-start.5 = (f32[64,128]{1,0:T(8,128)S(1)}, f32[64,128]{1,0:T(8,128)S(1)}, u32[]{:S(2)}, u32[]{:S(2)}) collective-permute-start(f32[64,128]{1,0:T(8,128)S(1)} %slice.17), channel_id=1, source_target_pairs={{0,4},{4,0},{8,12},{12,8},{16,20},{20,16},{24,28},{28,24},{32,36},... | collective-permute-start | bytes 98312 | tf_op jit(solution)/shard_map/ppermute | solution.py:263
  28.9 0.7 %collective-permute-done.5.refs_9_ = f32[64,128]{1,0:T(8,128)S(1)} collective-permute-done((f32[64,128]{1,0:T(8,128)S(1)}, f32[64,128]{1,0:T(8,128)S(1)}, u32[]{:S(2)}, u32[]{:S(2)}) %collective-permute-start.5) | collective-permute-done | bytes 32800 | tf_op jit(solution)/shard_map/ppermute | solution.py:263
  29.6 3.3 %shard_map.125 = (f32[40,512]{1,0:T(8,128)S(1)}, f32[24,512]{1,0:T(8,128)S(1)}, f32[24,128]{1,0:T(8,128)S(1)}, f32[24,128]{1,0:T(8,128)S(1)}) custom-call(s32[1]{0:T(128)} %bitcast.parity_ref.refs_0_, s32[1]{0:T(128)S(6)} %copy.13.count_ref.refs_1_, f32[40,512]{1,0:T(8,128)S(1)} %get-tuple-element.16.wide_ref.refs_2_, ...), custom_call_target="tpu_custom_call" | custom-call | tf_op jit(solution)/shard_map/pallas_call | solution.py:234
  33.3 1.3 %collective-permute-start.14 = (f32[24,512]{1,0:T(8,128)S(1)}, f32[24,512]{1,0:T(8,128)S(1)}, u32[]{:S(2)}, u32[]{:S(2)}) collective-permute-start(f32[24,512]{1,0:T(8,128)S(1)} %get-tuple-element.29.mine_ref), channel_id=1, source_target_pairs={{0,2},{1,3},{2,0},{3,1},{4,6},{5,7},{6,4},{7,5},{8,10},{9,11},{10,... | collective-permute-start | bytes 147464 | tf_op jit(solution)/shard_map/ppermute | solution.py:267
  34.6 3.5 %collective-permute-done.9.cross_in.refs_4_ = f32[48,128]{1,0:T(8,128)S(1)} collective-permute-done((f32[48,128]{1,0:T(8,128)S(1)}, f32[48,128]{1,0:T(8,128)S(1)}, u32[]{:S(2)}, u32[]{:S(2)}) %collective-permute-start.9) | collective-permute-done | bytes 24608 | tf_op jit(solution)/shard_map/ppermute | solution.py:262
  38.2 3.5 %collective-permute-start.10 = (f32[24,128]{1,0:T(8,128)S(1)}, f32[24,128]{1,0:T(8,128)S(1)}, u32[]{:S(2)}, u32[]{:S(2)}) collective-permute-start(f32[24,128]{1,0:T(8,128)S(1)} %slice.18), channel_id=1, source_target_pairs={{0,4},{4,0},{8,12},{12,8},{16,20},{20,16},{24,28},{28,24},{32,36},... | collective-permute-start | bytes 36872 | tf_op jit(solution)/shard_map/ppermute | solution.py:263
  41.7 0.8 %collective-permute-done.10.relay_in.refs_5_ = f32[24,128]{1,0:T(8,128)S(1)} collective-permute-done((f32[24,128]{1,0:T(8,128)S(1)}, f32[24,128]{1,0:T(8,128)S(1)}, u32[]{:S(2)}, u32[]{:S(2)}) %collective-permute-start.10) | collective-permute-done | bytes 12320 | tf_op jit(solution)/shard_map/ppermute | solution.py:263
  42.5 2.3 %shard_map.126 = (bf16[120,512]{1,0:T(8,128)(2,1)S(1)}, f32[64,128]{1,0:T(8,128)S(1)}, f32[64,128]{1,0:T(8,128)S(1)}) custom-call(s32[1]{0:T(128)} %bitcast.parity_ref.refs_0_, s32[1]{0:T(128)S(6)} %copy.13.count_ref.refs_1_, f32[40,512]{1,0:T(8,128)S(1)} %get-tuple-element.23.wide_ref.refs_2_, f32[24,128]{1,0:T(8,128)S(1)} %collective-permute-done.8.near_in.refs_3_, ...), custom_call_target="tpu_custom_call" | custom-call | tf_op jit(solution)/shard_map/pallas_call | solution.py:234
  45.6 0.5 collective-permute-done.11.refs_7_
  46.2 4.0 %collective-permute-done.12.refs_8_ = f32[128,128]{1,0:T(8,128)S(1)} collective-permute-done((f32[128,128]{1,0:T(8,128)S(1)}, f32[128,128]{1,0:T(8,128)S(1)}, u32[]{:S(2)}, u32[]{:S(2)}) %collective-permute-start.12) | collective-permute-done | bytes 65568 | tf_op jit(solution)/shard_map/ppermute | solution.py:262
  50.1 3.4 %collective-permute-start.13 = (f32[64,128]{1,0:T(8,128)S(1)}, f32[64,128]{1,0:T(8,128)S(1)}, u32[]{:S(2)}, u32[]{:S(2)}) collective-permute-start(f32[64,128]{1,0:T(8,128)S(1)} %slice.19), channel_id=1, source_target_pairs={{0,4},{4,0},{8,12},{12,8},{16,20},{20,16},{24,28},{28,24},{32,36},... | collective-permute-start | bytes 98312 | tf_op jit(solution)/shard_map/ppermute | solution.py:263
  53.7 0.7 %collective-permute-done.13.refs_9_ = f32[64,128]{1,0:T(8,128)S(1)} collective-permute-done((f32[64,128]{1,0:T(8,128)S(1)}, f32[64,128]{1,0:T(8,128)S(1)}, u32[]{:S(2)}, u32[]{:S(2)}) %collective-permute-start.13) | collective-permute-done | bytes 32800 | tf_op jit(solution)/shard_map/ppermute | solution.py:263
  54.4 3.8 %shard_map.128 = (f32[5,4,512]{2,1,0:T(4,128)}, f32[5,4,512]{2,1,0:T(4,128)}) custom-call(s32[1]{0:T(128)} %bitcast.parity_ref.refs_0_, s32[1]{0:T(128)S(6)} %copy.13.count_ref.refs_1_, f32[40,512]{1,0:T(8,128)S(1)} %get-tuple-element.23.wide_ref.refs_2_, f32[24,128]{1,0:T(8,128)S(1)} %collective-permute-done.8.near_in.refs_3_, ...), custom_call_target="tpu_custom_call" | custom-call | tf_op jit(solution)/shard_map/pallas_call | solution.py:234
  (47 shorter events, 2.6 us)
Async XLA Ops:
  2.4 4.5 %collective-permute-start = (f32[24,128]{1,0:T(8,128)S(1)}, f32[24,128]{1,0:T(8,128)S(1)}, u32[]{:S(2)}, u32[]{:S(2)}) collective-permute-start(f32[24,128]{1,0:T(8,128)S(1)} %get-tuple-element.17), channel_id=1, source_target_pairs={{0,4},{4,0},{8,12},{12,8},{16,20},{20,16},{24,28},{28,24},{32,36},... | collective-permute-start | bytes 36872 | tf_op jit(solution)/shard_map/ppermute | solution.py:260
  5.7 14.7 %collective-permute-start.6 = (f32[24,512]{1,0:T(8,128)S(1)}, f32[24,512]{1,0:T(8,128)S(1)}, u32[]{:S(2)}, u32[]{:S(2)}) collective-permute-start(f32[24,512]{1,0:T(8,128)S(1)} %get-tuple-element.22.mine_ref), channel_id=1, source_target_pairs={{0,2},{1,3},{2,0},{3,1},{4,6},{5,7},{6,4},{7,5},{8,10},{9,11},{10,... | collective-permute-start | bytes 147464 | tf_op jit(solution)/shard_map/ppermute | solution.py:267
  6.9 10.7 %copy-start = (f32[3,2048]{1,0:T(4,128)S(1)}, f32[3,2048]{1,0:T(4,128)}, u32[]{:S(2)}) copy-start(f32[3,2048]{1,0:T(4,128)} %refs_12_.3) | copy-start | bytes 73732
  6.9 3.6 %collective-permute-start.1 = (f32[48,128]{1,0:T(8,128)S(1)}, f32[48,128]{1,0:T(8,128)S(1)}, u32[]{:S(2)}, u32[]{:S(2)}) collective-permute-start(f32[48,128]{1,0:T(8,128)S(1)} %pad_maximum_fusion.4), channel_id=1, source_target_pairs={{4,8},{12,16},{20,24},{28,32},{36,40},{44,48},{52,56},{60,64},{68,... | collective-permute-start | bytes 73736 | tf_op jit(solution)/shard_map/ppermute | solution.py:262
  10.5 7.1 %copy-start.5 = (s32[2048]{0:T(1024)S(1)}, s32[2048]{0:T(1024)}, u32[]{:S(2)}) copy-start(s32[2048]{0:T(1024)} %param.18) | copy-start | bytes 24580
  10.5 7.1 %copy-start.8 = (f32[512]{0:T(512)S(1)}, f32[512]{0:T(512)}, u32[]{:S(2)}) copy-start(f32[512]{0:T(512)} %param.12) | copy-start | bytes 6148
  10.5 7.1 %copy-start.4 = (s32[2048]{0:T(1024)S(1)}, s32[2048]{0:T(1024)}, u32[]{:S(2)}) copy-start(s32[2048]{0:T(1024)} %param.17) | copy-start | bytes 24580
  10.5 7.1 %collective-permute-start.2 = (f32[24,128]{1,0:T(8,128)S(1)}, f32[24,128]{1,0:T(8,128)S(1)}, u32[]{:S(2)}, u32[]{:S(2)}) collective-permute-start(f32[24,128]{1,0:T(8,128)S(1)} %slice.16), channel_id=1, source_target_pairs={{0,4},{4,0},{8,12},{12,8},{16,20},{20,16},{24,28},{28,24},{32,36},... | collective-permute-start | bytes 36872 | tf_op jit(solution)/shard_map/ppermute | solution.py:263
  20.0 1.3 %collective-permute-start.3 = (f32[64,128]{1,0:T(8,128)S(1)}, f32[64,128]{1,0:T(8,128)S(1)}, u32[]{:S(2)}, u32[]{:S(2)}) collective-permute-start(f32[64,128]{1,0:T(8,128)S(1)} %get-tuple-element.20), channel_id=1, source_target_pairs={{0,4},{4,0},{8,12},{12,8},{16,20},{20,16},{24,28},{28,24},{32,36},... | collective-permute-start | bytes 98312 | tf_op jit(solution)/shard_map/ppermute | solution.py:260
  20.4 8.3 %collective-permute-start.7 = (f32[48,512]{1,0:T(8,128)S(1)}, f32[48,512]{1,0:T(8,128)S(1)}, u32[]{:S(2)}, u32[]{:S(2)}) collective-permute-start(f32[48,512]{1,0:T(8,128)S(1)} %pad_maximum_fusion), channel_id=1, source_target_pairs={{0,1},{1,0},{2,3},{3,2},{4,5},{5,4},{6,7},{7,6},{8,9},{9,8},{10,11... | collective-permute-start | bytes 294920 | tf_op jit(solution)/shard_map/ppermute | solution.py:269
  21.3 7.5 %copy-start.1 = (f32[4,40,96]{2,1,0:T(8,128)S(1)}, f32[4,40,96]{2,1,0:T(8,128)}, u32[]{:S(2)}) copy-start(f32[4,40,96]{2,1,0:T(8,128)} %constant.13.clone.matrix_ref) | copy-start | bytes 184324
  21.3 4.0 %collective-permute-start.4 = (f32[128,128]{1,0:T(8,128)S(1)}, f32[128,128]{1,0:T(8,128)S(1)}, u32[]{:S(2)}, u32[]{:S(2)}) collective-permute-start(f32[128,128]{1,0:T(8,128)S(1)} %pad_maximum_fusion.2), channel_id=1, source_target_pairs={{4,8},{12,16},{20,24},{28,32},{36,40},{44,48},{52,56},{60,64},{68,... | collective-permute-start | bytes 196616 | tf_op jit(solution)/shard_map/ppermute | solution.py:262
  25.3 4.3 %collective-permute-start.5 = (f32[64,128]{1,0:T(8,128)S(1)}, f32[64,128]{1,0:T(8,128)S(1)}, u32[]{:S(2)}, u32[]{:S(2)}) collective-permute-start(f32[64,128]{1,0:T(8,128)S(1)} %slice.17), channel_id=1, source_target_pairs={{0,4},{4,0},{8,12},{12,8},{16,20},{20,16},{24,28},{28,24},{32,36},... | collective-permute-start | bytes 98312 | tf_op jit(solution)/shard_map/ppermute | solution.py:263
  28.7 0.9 %copy-start.6 = (f32[3,2048]{1,0:T(4,128)S(1)}, f32[3,2048]{1,0:T(4,128)}, u32[]{:S(2)}) copy-start(f32[3,2048]{1,0:T(4,128)} %refs_13_.3) | copy-start | bytes 73732
  28.7 0.9 %copy-start.7 = (f32[3,2048]{1,0:T(4,128)S(1)}, f32[3,2048]{1,0:T(4,128)}, u32[]{:S(2)}) copy-start(f32[3,2048]{1,0:T(4,128)} %refs_14_.3) | copy-start | bytes 73732
  32.9 1.7 %collective-permute-start.8 = (f32[24,128]{1,0:T(8,128)S(1)}, f32[24,128]{1,0:T(8,128)S(1)}, u32[]{:S(2)}, u32[]{:S(2)}) collective-permute-start(f32[24,128]{1,0:T(8,128)S(1)} %get-tuple-element.24), channel_id=1, source_target_pairs={{0,4},{4,0},{8,12},{12,8},{16,20},{20,16},{24,28},{28,24},{32,36},... | collective-permute-start | bytes 36872 | tf_op jit(solution)/shard_map/ppermute | solution.py:260
  33.3 12.0 %collective-permute-start.14 = (f32[24,512]{1,0:T(8,128)S(1)}, f32[24,512]{1,0:T(8,128)S(1)}, u32[]{:S(2)}, u32[]{:S(2)}) collective-permute-start(f32[24,512]{1,0:T(8,128)S(1)} %get-tuple-element.29.mine_ref), channel_id=1, source_target_pairs={{0,2},{1,3},{2,0},{3,1},{4,6},{5,7},{6,4},{7,5},{8,10},{9,11},{10,... | collective-permute-start | bytes 147464 | tf_op jit(solution)/shard_map/ppermute | solution.py:267
  34.6 3.5 %collective-permute-start.9 = (f32[48,128]{1,0:T(8,128)S(1)}, f32[48,128]{1,0:T(8,128)S(1)}, u32[]{:S(2)}, u32[]{:S(2)}) collective-permute-start(f32[48,128]{1,0:T(8,128)S(1)} %pad_maximum_fusion.5), channel_id=1, source_target_pairs={{4,8},{12,16},{20,24},{28,32},{36,40},{44,48},{52,56},{60,64},{68,... | collective-permute-start | bytes 73736 | tf_op jit(solution)/shard_map/ppermute | solution.py:262
  38.2 4.3 %collective-permute-start.10 = (f32[24,128]{1,0:T(8,128)S(1)}, f32[24,128]{1,0:T(8,128)S(1)}, u32[]{:S(2)}, u32[]{:S(2)}) collective-permute-start(f32[24,128]{1,0:T(8,128)S(1)} %slice.18), channel_id=1, source_target_pairs={{0,4},{4,0},{8,12},{12,8},{16,20},{20,16},{24,28},{28,24},{32,36},... | collective-permute-start | bytes 36872 | tf_op jit(solution)/shard_map/ppermute | solution.py:263
  44.8 1.3 %collective-permute-start.11 = (f32[64,128]{1,0:T(8,128)S(1)}, f32[64,128]{1,0:T(8,128)S(1)}, u32[]{:S(2)}, u32[]{:S(2)}) collective-permute-start(f32[64,128]{1,0:T(8,128)S(1)} %get-tuple-element.27), channel_id=1, source_target_pairs={{0,4},{4,0},{8,12},{12,8},{16,20},{20,16},{24,28},{28,24},{32,36},... | collective-permute-start | bytes 98312 | tf_op jit(solution)/shard_map/ppermute | solution.py:260
  45.3 8.2 %collective-permute-start.15 = (f32[48,512]{1,0:T(8,128)S(1)}, f32[48,512]{1,0:T(8,128)S(1)}, u32[]{:S(2)}, u32[]{:S(2)}) collective-permute-start(f32[48,512]{1,0:T(8,128)S(1)} %pad_maximum_fusion.1), channel_id=1, source_target_pairs={{0,1},{1,0},{2,3},{3,2},{4,5},{5,4},{6,7},{7,6},{8,9},{9,8},{10,11... | collective-permute-start | bytes 294920 | tf_op jit(solution)/shard_map/ppermute | solution.py:269
  46.1 4.0 %collective-permute-start.12 = (f32[128,128]{1,0:T(8,128)S(1)}, f32[128,128]{1,0:T(8,128)S(1)}, u32[]{:S(2)}, u32[]{:S(2)}) collective-permute-start(f32[128,128]{1,0:T(8,128)S(1)} %pad_maximum_fusion.3), channel_id=1, source_target_pairs={{4,8},{12,16},{20,24},{28,32},{36,40},{44,48},{52,56},{60,64},{68,... | collective-permute-start | bytes 196616 | tf_op jit(solution)/shard_map/ppermute | solution.py:262
  50.1 4.2 %copy-start.3 = (f32[5,4,512]{2,1,0:T(4,128)S(1)}, f32[5,4,512]{2,1,0:T(4,128)}, u32[]{:S(2)}) copy-start(f32[5,4,512]{2,1,0:T(4,128)} %refs_18_.3) | copy-start | bytes 122884
  50.1 4.2 %collective-permute-start.13 = (f32[64,128]{1,0:T(8,128)S(1)}, f32[64,128]{1,0:T(8,128)S(1)}, u32[]{:S(2)}, u32[]{:S(2)}) collective-permute-start(f32[64,128]{1,0:T(8,128)S(1)} %slice.19), channel_id=1, source_target_pairs={{0,4},{4,0},{8,12},{12,8},{16,20},{20,16},{24,28},{28,24},{32,36},... | collective-permute-start | bytes 98312 | tf_op jit(solution)/shard_map/ppermute | solution.py:263
  (3 other events, 2.2 us)

commit v2 on v1

--- a/solution.py
+++ b/solution.py
@@ -20,6 +20,10 @@
 F32 = jnp.float32
 
 
+def parity_of_partition():
+    return lax.axis_index("dom") & 1
+
+
 def top_rows(shape):
     return (lax.broadcasted_iota(jnp.int32, shape, 0) & 7) < 4
 
@@ -47,7 +51,7 @@
 
 def one_hot(ids, rows):
     cell = lax.broadcasted_iota(jnp.int32, (rows, ids.shape[1]), 0)
-    return jnp.where(cell == ids, 1.0, 0.0).astype(F32)
+    return jnp.where(cell == ids, 1.0, 0.0)
 
 
 def paired(groups):
@@ -93,37 +97,55 @@
     return pieces(unpaired(jnp.concatenate([left, right], axis=1), count))
 
 
-def send_kernel(parity_ref, state_ref, send_ref, near_ref, far_ref, wide_ref, dense_ref):
+def send_kernel(
+    state_hbm, send_hbm, near_ref, far_ref, wide_ref, dense_ref, state_ref, send_ref, state_sem, send_sem
+):
+    fetch_state = pltpu.make_async_copy(state_hbm, state_ref, state_sem)
+    fetch_send = pltpu.make_async_copy(send_hbm, send_ref, send_sem)
+    fetch_state.start()
+    fetch_send.start()
+    fetch_send.wait()
+    fetch_state.wait()
     for v in range(NV):
         wide_ref[8 * v : 8 * v + 4, :] = state_ref[v]
         wide_ref[8 * v + 4 : 8 * v + 8, :] = state_ref[v]
     wide = wide_ref[...]
-    write_messages(pieces(wide), send_ref[...], parity_ref[0], near_ref, far_ref)
+    write_messages(pieces(wide), send_ref[...], parity_of_partition(), near_ref, far_ref)
     dense_ref[...] = paired([wide[8 * v : 8 * v + 8] for v in range(NV)])
 
 
+def hot_kernel(owner_ref, neighbor_ref, own_ref, other_ref):
+    for f in range(0, FACES, CHUNK):
+        faces = slice(f, f + CHUNK)
+        own_ref[:, faces] = one_hot(owner_ref[:, faces], CELLS).astype(BF)
+        other_ref[:, faces] = one_hot(neighbor_ref[:, faces], CELLS + GHOSTS).astype(BF)
+
+
+def jump_kernel(wide_ref, own_ref, other_ref, jump_ref):
+    values = pieces(wide_ref[...])
+    for f in range(0, FACES, CHUNK):
+        faces = slice(f, f + CHUNK)
+        jump_ref[:, faces] = matmul(values, other_ref[:CELLS, faces] - own_ref[:, faces])
+
+
 def gradient_kernel(
-    parity_ref, count_ref, wide_ref, near_in, cross_in, relay_in, owner_ref, neighbor_ref, normal_ref,
-    volume_ref, send_ref, table_ref, near_ref, far_ref,
+    count_ref, jump_ref, near_in, cross_in, relay_in, own_ref, other_ref, normal_ref, volume_ref, send_ref,
+    table_ref, near_ref, far_ref,
 ):
-    parity = parity_ref[0]
+    parity = parity_of_partition()
     ghosts = ghost_table(near_in[...], cross_in[...], relay_in[...], parity, NV)
-    values = jnp.concatenate([pieces(wide_ref[...]), ghosts], axis=1)
     total = jnp.zeros((GROWS, CELLS), F32)
     for f in range(0, FACES, CHUNK):
-        own = one_hot(owner_ref[:, f : f + CHUNK], CELLS)
-        other = one_hot(neighbor_ref[:, f : f + CHUNK], CELLS + GHOSTS)
-        local = other[:CELLS]
-        jump_hot = jnp.concatenate([local - own, other[CELLS:]], axis=0).astype(BF)
-        sum_hot = (local + own).astype(BF)
-        jump = matmul(values, jump_hot)
+        faces = slice(f, f + CHUNK)
+        jump = jump_ref[:, faces] + matmul(ghosts, other_ref[CELLS:, faces])
         jumps = [fold(jump[8 * v : 8 * v + 8]) for v in range(NV)]
         live = lax.broadcasted_iota(jnp.int32, (1, CHUNK), 1) + f < count_ref[0]
         flows = []
         for d in range(3):
-            half = jnp.where(live, 0.5 * normal_ref[d : d + 1, f : f + CHUNK], 0.0)
+            half = jnp.where(live, 0.5 * normal_ref[d : d + 1, faces], 0.0)
             for v in range(NV):
                 flows.append(jumps[v] * half)
+        sum_hot = other_ref[:CELLS, faces] + own_ref[:, faces]
         total = total + matmul_t(pieces(jnp.concatenate(flows, axis=0)), sum_hot)
     inverse = 1.0 / volume_ref[...]
     gradient = jnp.concatenate([fold(total[8 * g : 8 * g + 8]) * inverse for g in range(3 * NV)], axis=0)
@@ -132,35 +154,48 @@
     write_messages(table, send_ref[...], parity, near_ref, far_ref)
 
 
+def with_arms(values, arm_ref, faces):
+    arms = [arm_ref[d : d + 1, faces] for d in range(3)]
+    out = []
+    for v in range(NV):
+        total = values[8 * v : 8 * v + 8]
+        for d in range(3):
+            g = VROWS + 8 * (NV * d + v)
+            total = total + values[g : g + 8] * arms[d]
+        out.append(total)
+    return out
+
+
+def face_kernel(wide_ref, table_ref, own_ref, other_ref, owner_arm_ref, neighbor_arm_ref, face_ref):
+    values = jnp.concatenate([pieces(wide_ref[...]), table_ref[...]], axis=0)
+    top = top_rows((8, CHUNK))
+    for f in range(0, FACES, CHUNK):
+        faces = slice(f, f + CHUNK)
+        left = with_arms(matmul(values, own_ref[:, faces]), owner_arm_ref, faces)
+        right = with_arms(matmul(values, other_ref[:CELLS, faces]), neighbor_arm_ref, faces)
+        for v in range(NV):
+            a, b = left[v], right[v]
+            face_ref[8 * v : 8 * v + 8, faces] = jnp.where(top, a, b) + swap_halves(jnp.where(top, b, a))
+
+
 def spatial_groups(
-    parity_ref, count_ref, wide_ref, near_in, cross_in, relay_in, table_ref, gnear_in, gcross_in, grelay_in,
-    owner_ref, neighbor_ref, normal_ref, owner_arm_ref, neighbor_arm_ref, volume_ref,
+    count_ref, face_ref, near_in, cross_in, relay_in, gnear_in, gcross_in, grelay_in, own_ref, other_ref,
+    normal_ref, neighbor_arm_ref, volume_ref,
 ):
-    parity = parity_ref[0]
+    parity = parity_of_partition()
     ghosts = ghost_table(near_in[...], cross_in[...], relay_in[...], parity, NV)
     grad_ghosts = ghost_table(gnear_in[...], gcross_in[...], grelay_in[...], parity, 3 * NV)
-    local = jnp.concatenate([pieces(wide_ref[...]), table_ref[...]], axis=0)
-    values = jnp.concatenate([local, jnp.concatenate([ghosts, grad_ghosts], axis=0)], axis=1)
+    values = jnp.concatenate([ghosts, grad_ghosts], axis=0)
     total = jnp.zeros((VROWS, CELLS), F32)
     top = top_rows((8, CHUNK))
     sign = jnp.where(top, 1.0, -1.0)
     for f in range(0, FACES, CHUNK):
-        own = one_hot(owner_ref[:, f : f + CHUNK], CELLS)
-        other = one_hot(neighbor_ref[:, f : f + CHUNK], CELLS + GHOSTS)
-        difference = (own - other[:CELLS]).astype(BF)
-        left = matmul(local, own.astype(BF))
-        right = matmul(values, other.astype(BF))
+        faces = slice(f, f + CHUNK)
+        right = with_arms(matmul(values, other_ref[CELLS:, faces]), neighbor_arm_ref, faces)
         live = lax.broadcasted_iota(jnp.int32, (1, CHUNK), 1) + f < count_ref[0]
-        normals = [jnp.where(live, normal_ref[d : d + 1, f : f + CHUNK], 0.0) for d in range(3)]
+        normals = [jnp.where(live, normal_ref[d : d + 1, faces], 0.0) for d in range(3)]
         area = jnp.sqrt(normals[0] * normals[0] + normals[1] * normals[1] + normals[2] * normals[2])
-        states = []
-        for v in range(NV):
-            a, b = left[8 * v : 8 * v + 8], right[8 * v : 8 * v + 8]
-            for d in range(3):
-                g = VROWS + 8 * (NV * d + v)
-                a = a + left[g : g + 8] * owner_arm_ref[d : d + 1, f : f + CHUNK]
-                b = b + right[g : g + 8] * neighbor_arm_ref[d : d + 1, f : f + CHUNK]
-            states.append(jnp.where(top, a, b) + swap_halves(jnp.where(top, b, a)))
+        states = [face_ref[8 * v : 8 * v + 8, faces] + jnp.where(top, 0.0, fold(right[v])) for v in range(NV)]
         density, energy = states[0], states[4]
         momentum = states[1:4]
         inverse = 1.0 / density
@@ -174,16 +209,16 @@
         for d in range(3):
             flux.append(momentum[d] * speed + pressure * normals[d])
         flux.append((energy + pressure) * speed)
-        faces = [fold(0.5 * (flux[v] + wave * states[v])) for v in range(NV)]
-        total = total + matmul_t(pieces(jnp.concatenate(faces, axis=0)), difference)
+        fluxes = [fold(0.5 * (flux[v] + wave * states[v])) for v in range(NV)]
+        difference = own_ref[:, faces] - other_ref[:CELLS, faces]
+        total = total + matmul_t(pieces(jnp.concatenate(fluxes, axis=0)), difference)
     inverse = 1.0 / volume_ref[...]
     return [fold(total[8 * v : 8 * v + 8]) * inverse for v in range(NV)]
 
 
 def middle_kernel(*refs):
-    *common, spectral_ref, step_ref, send_ref, wide_out, dense_ref, near_ref, far_ref = refs
+    *common, spectral_ref, step_ref, wide_ref, send_ref, wide_out, dense_ref, near_ref, far_ref = refs
     spatial = spatial_groups(*common)
-    wide_ref, parity = common[2], common[0][0]
     groups = []
     for v in range(NV):
         rows = slice(8 * v, 8 * v + 8)
@@ -191,7 +226,7 @@
     wide = jnp.concatenate(groups, axis=0)
     wide_out[...] = wide
     dense_ref[...] = paired(groups)
-    write_messages(pieces(wide), send_ref[...], parity, near_ref, far_ref)
+    write_messages(pieces(wide), send_ref[...], parity_of_partition(), near_ref, far_ref)
 
 
 def last_kernel(*refs):
@@ -203,8 +238,8 @@
         new_ref[v] = state_ref[v] - step_ref[...] * rate
 
 
-def spectral_kernel(index_ref, matrix_ref, mine_ref, next_ref, rest_ref, out_ref):
-    matrix = matrix_ref[index_ref[0]]
+def spectral_kernel(matrix_ref, mine_ref, next_ref, rest_ref, out_ref):
+    matrix = matrix_ref[lax.axis_index("inst")]
     data = jnp.concatenate([mine_ref[...], next_ref[...], rest_ref[...]], axis=0)
     m_high, d_high = matrix.astype(BF), data.astype(BF)
     m_low, d_low = (matrix - m_high.astype(F32)).astype(BF), (data - d_high.astype(F32)).astype(BF)
@@ -224,19 +259,21 @@
                 for b in range(groups):
                     for t in range(size):
                         column = b * 24 + (v // 2) * 8 + (v % 2) * 4 + t
-                        out[y, 8 * v + s, column] = table[size * y + s % size, size * (y ^ (0, 2, 1, 3)[b]) + t]
+                        out[y, 8 * v + s, column] = table[size * y + s % size, size * (y ^ (0, 1, 3, 2)[b]) + t]
     return out
 
 
-def call(kernel, outputs, scalars, arrays):
+def call(kernel, outputs, scalars, arrays, hbm=0, scratch=(), limit=8):
     smem = pl.BlockSpec(memory_space=pltpu.SMEM)
     vmem = pl.BlockSpec(memory_space=pltpu.VMEM)
+    far = pl.BlockSpec(memory_space=pltpu.HBM)
     return pl.pallas_call(
         kernel,
         out_shape=[jax.ShapeDtypeStruct(s, d) for s, d in outputs],
-        in_specs=[smem] * len(scalars) + [vmem] * len(arrays),
+        in_specs=[smem] * len(scalars) + [far] * hbm + [vmem] * (len(arrays) - hbm),
         out_specs=[vmem] * len(outputs),
-        compiler_params=pltpu.CompilerParams(vmem_limit_bytes=32 << 20),
+        scratch_shapes=scratch,
+        compiler_params=pltpu.CompilerParams(vmem_limit_bytes=limit << 20),
     )(*scalars, *arrays)
 
 
@@ -245,9 +282,6 @@
     send_cells,
 ):
     parts = lax.axis_size("dom")
-    place = lax.axis_index("dom")
-    parity = (place & 1).astype(jnp.int32).reshape(1)
-    line = lax.axis_index("inst").astype(jnp.int32).reshape(1)
     volume = cell_volume.reshape(1, CELLS)
     step = step_size.reshape(1, CELLS)
     owner = face_owner.reshape(1, FACES)
@@ -264,33 +298,42 @@
         return got, cross, relay
 
     def instances(dense):
-        one = lax.ppermute(dense, "inst", [(i, i ^ 2) for i in range(4)])
+        one = lax.ppermute(dense, "inst", [(i, i ^ 1) for i in range(4)])
         outgoing = jnp.concatenate([dense, one], axis=0)
-        two = lax.ppermute(outgoing, "inst", [(i, i ^ 1) for i in range(4)])
-        return call(spectral_kernel, [((VROWS, CELLS), F32)], [line], [matrices, dense, one, two])[0]
+        rest = lax.ppermute(outgoing, "inst", [(i, i ^ 3) for i in range(4)])
+        arrays = [matrices, dense, one, rest]
+        return call(spectral_kernel, [((VROWS, CELLS), F32)], [], arrays)[0]
 
     def message(rows):
         return [((rows, 128), F32)] * 2
 
     wide_shape, dense_shape = ((VROWS, CELLS), F32), ((24, CELLS), F32)
-    geometry = [owner, neighbor, face_normal]
-    arms = [owner_arm, neighbor_arm, volume]
-    near, far, wide, dense = call(send_kernel, message(24) + [wide_shape, dense_shape], [parity], [state, send_cells])
+    faces_shape = ((VROWS, FACES), F32)
+    near, far, wide, dense = call(
+        send_kernel, message(24) + [wide_shape, dense_shape], [], [state, send_cells], hbm=2,
+        scratch=[
+            pltpu.VMEM(state.shape, F32), pltpu.VMEM(send_cells.shape, jnp.int32), pltpu.SemaphoreType.DMA,
+            pltpu.SemaphoreType.DMA,
+        ],
+    )
+    hot = call(hot_kernel, [((CELLS, FACES), BF), ((CELLS + GHOSTS, FACES), BF)], [], [owner, neighbor])
     for section in range(2):
+        jump = call(jump_kernel, [faces_shape], [], [wide, *hot])[0]
         ghosts = exchange(near, far)
         spectral = instances(dense)
         table, gnear, gfar = call(
-            gradient_kernel, [((GROWS, CELLS), BF)] + message(64), [parity, face_count],
-            [wide, *ghosts, *geometry, volume, send_cells],
+            gradient_kernel, [((GROWS, CELLS), BF)] + message(64), [face_count],
+            [jump, *ghosts, *hot, face_normal, volume, send_cells],
         )
+        face = call(face_kernel, [faces_shape], [], [wide, table, *hot, owner_arm, neighbor_arm])[0]
         gradient_ghosts = exchange(gnear, gfar)
-        common = [wide, *ghosts, table, *gradient_ghosts, *geometry, *arms, spectral, step]
+        common = [face, *ghosts, *gradient_ghosts, *hot, face_normal, neighbor_arm, volume, spectral, step]
         if section == 0:
             wide, dense, near, far = call(
-                middle_kernel, [wide_shape, dense_shape] + message(24), [parity, face_count], [*common, send_cells],
+                middle_kernel, [wide_shape, dense_shape] + message(24), [face_count],
+                [*common, wide, send_cells],
             )
-    shape = state.shape
-    return tuple(call(last_kernel, [(shape, F32)] * 2, [parity, face_count], [*common, state]))
+    return tuple(call(last_kernel, [(state.shape, F32)] * 2, [face_count], [*common, state]))
 
 
 def solution(mesh):

time: 58.4 us -> 55.7 us (0.954)
  starting transfers between devices: 26 us -> 23.5 us
  Pallas kernels: 12.4 us -> 11 us
  local copies, waits for them, and re-layouts: 1.53 us -> 2.9 us
    ppermute x4, waiting for transfers between devices: 2.35 us -> 0.39 us  [exchange(): relay = lax.ppermute(cross[:far.shape[0]], 'dom', inside)]
    unnamed x22 -> x24, local copies, waits for them, and re-layouts: 1.52 us -> 2.89 us
    pallas_call x7 -> x12, Pallas kernels: 12.4 us -> 11 us  [call(): pl.pallas_call(kernel, out_shape=[jax.ShapeDtypeStruct(s, d) for s, d in...]
    ppermute x4, waiting for transfers between devices: 0.9 us -> 2.17 us  [exchange(): got = lax.ppermute(near, 'dom', inside)]
    ppermute x4, starting transfers between devices: 1.66 us -> 0.42 us  [exchange(): cross = lax.ppermute(outgoing, 'dom', across)]
    ppermute x4, starting transfers between devices: 4.57 us -> 3.92 us  [exchange(): got = lax.ppermute(near, 'dom', inside)]
  transfers between devices with their start and end apart: 16 -> 16, of which waited for: 10 -> 8; matrix products, arithmetic and copies ran while one was open for 0% -> 0% of each run, Pallas kernels for 9% -> 13%
where the time goes in v2:
time: 55.7 us; the launch traced here: 55.5 us
  starting transfers between devices  23.5 us (42%)
  waiting for transfers between devices  16.5 us (30%)
  Pallas kernels  11 us (20%)
  local copies, waits for them, and re-layouts  2.9 us (5%)
  between operations  1.54 us (3%)
    ppermute x4, starting transfers between devices, exchange(): relay = lax.ppermute(cross[:far.shape[0]], 'dom', inside)  16.1 us
    ppermute x4, waiting for transfers between devices, exchange(): cross = lax.ppermute(outgoing, 'dom', across)  13.9 us
    pallas_call x12, Pallas kernels, call(): pl.pallas_call(kernel, out_shape=[jax.ShapeDtypeStruct(s, d) for s, d in...  11 us
    ppermute x4, starting transfers between devices, exchange(): got = lax.ppermute(near, 'dom', inside)  3.92 us
    ppermute x2, starting transfers between devices, instances(): rest = lax.ppermute(outgoing, 'inst', [(i, i ^ 3) for i in range(4)])  2.92 us
    unnamed x24, local copies, waits for them, and re-layouts  2.89 us
    ppermute x4, waiting for transfers between devices, exchange(): got = lax.ppermute(near, 'dom', inside)  2.17 us
  transfers between devices with their start and end apart: 16, of which 8 were waited for; matrix products, arithmetic and copies ran while one was open for 0% of the time, Pallas kernels for 13%

profile of v2, /device:TPU:1, one launch (start us, length us, event | category | flops | bytes accessed | tf_op | source)
XLA Modules:
  0.0 55.5 jit_solution(6285076265415199672)
XLA Ops:
  0.7 0.8 %copy-done.3 = f32[5,4,512]{2,1,0:T(4,128)S(1)} copy-done((f32[5,4,512]{2,1,0:T(4,128)S(1)}, f32[5,4,512]{2,1,0:T(4,128)}, u32[]{:S(2)}) %copy-start.3) | copy-done | bytes 40984
  1.4 0.7 %copy-done.7 = s32[4,64]{1,0:T(4,128)S(1)} copy-done((s32[4,64]{1,0:T(4,128)S(1)}, s32[4,64]{1,0:T(4,128)}, u32[]{:S(2)}) %copy-start.7) | copy-done | bytes 1048
  2.5 3.3 %collective-permute-start = (f32[24,128]{1,0:T(8,128)S(1)}, f32[24,128]{1,0:T(8,128)S(1)}, u32[]{:S(2)}, u32[]{:S(2)}) collective-permute-start(f32[24,128]{1,0:T(8,128)S(1)} %get-tuple-element.21), channel_id=1, source_target_pairs={{0,4},{4,0},{8,12},{12,8},{16,20},{20,16},{24,28},{28,24},{32,36},... | collective-permute-start | bytes 36872 | tf_op jit(solution)/shard_map/ppermute | solution.py:294
  5.8 0.8 %collective-permute-done.near_in.refs_2_ = f32[24,128]{1,0:T(8,128)S(1)} collective-permute-done((f32[24,128]{1,0:T(8,128)S(1)}, f32[24,128]{1,0:T(8,128)S(1)}, u32[]{:S(2)}, u32[]{:S(2)}) %collective-permute-start) | collective-permute-done | bytes 12320 | tf_op jit(solution)/shard_map/ppermute | solution.py:294
  6.8 3.0 %collective-permute-done.1.cross_in.refs_3_ = f32[48,128]{1,0:T(8,128)S(1)} collective-permute-done((f32[48,128]{1,0:T(8,128)S(1)}, f32[48,128]{1,0:T(8,128)S(1)}, u32[]{:S(2)}, u32[]{:S(2)}) %collective-permute-start.1) | collective-permute-done | bytes 24608 | tf_op jit(solution)/shard_map/ppermute | solution.py:296
  9.8 5.2 %collective-permute-start.2 = (f32[24,128]{1,0:T(8,128)S(1)}, f32[24,128]{1,0:T(8,128)S(1)}, u32[]{:S(2)}, u32[]{:S(2)}) collective-permute-start(f32[24,128]{1,0:T(8,128)S(1)} %slice.16), channel_id=1, source_target_pairs={{0,4},{4,0},{8,12},{12,8},{16,20},{20,16},{24,28},{28,24},{32,36},... | collective-permute-start | bytes 36872 | tf_op jit(solution)/shard_map/ppermute | solution.py:297
  15.7 0.7 %copy-done.10 = s32[2048]{0:T(1024)S(1)} copy-done((s32[2048]{0:T(1024)S(1)}, s32[2048]{0:T(1024)}, u32[]{:S(2)}) %copy-start.10) | copy-done | bytes 8216
  16.4 0.7 %copy-done.11 = s32[2048]{0:T(1024)S(1)} copy-done((s32[2048]{0:T(1024)S(1)}, s32[2048]{0:T(1024)}, u32[]{:S(2)}) %copy-start.11) | copy-done | bytes 8216
  17.1 1.0 %shard_map.123 = (bf16[512,2048]{1,0:T(8,128)(2,1)S(1)}, bf16[768,2048]{1,0:T(8,128)(2,1)S(1)}) custom-call(s32[1,2048]{1,0:T(1,128)S(1)} %bitcast.10, s32[1,2048]{1,0:T(1,128)S(1)} %bitcast.11), custom_call_target="tpu_custom_call" | custom-call | tf_op jit(solution)/shard_map/pallas_call | solution.py:270
  18.6 1.4 %shard_map.125 = (bf16[120,512]{1,0:T(8,128)(2,1)S(1)}, f32[64,128]{1,0:T(8,128)S(1)}, f32[64,128]{1,0:T(8,128)S(1)}) custom-call(s32[1]{0:T(128)S(6)} %copy.13.count_ref.refs_0_, f32[40,2048]{1,0:T(8,128)S(1)} %shard_map.124.jump_ref, f32[24,128]{1,0:T(8,128)S(1)} %collective-permute-done.near_in.refs_2_, ...), custom_call_target="tpu_custom_call" | custom-call | tf_op jit(solution)/shard_map/pallas_call | solution.py:270
  20.2 2.4 %collective-permute-start.7 = (f32[48,512]{1,0:T(8,128)S(1)}, f32[48,512]{1,0:T(8,128)S(1)}, u32[]{:S(2)}, u32[]{:S(2)}) collective-permute-start(f32[48,512]{1,0:T(8,128)S(1)} %pad_maximum_fusion), channel_id=1, source_target_pairs={{0,3},{1,2},{2,1},{3,0},{4,7},{5,6},{6,5},{7,4},{8,11},{9,10},{10,... | collective-permute-start | bytes 294920 | tf_op jit(solution)/shard_map/ppermute | solution.py:303
  22.7 3.7 %collective-permute-done.4.refs_6_ = f32[128,128]{1,0:T(8,128)S(1)} collective-permute-done((f32[128,128]{1,0:T(8,128)S(1)}, f32[128,128]{1,0:T(8,128)S(1)}, u32[]{:S(2)}, u32[]{:S(2)}) %collective-permute-start.4) | collective-permute-done | bytes 65568 | tf_op jit(solution)/shard_map/ppermute | solution.py:296
  26.4 4.1 %collective-permute-start.5 = (f32[64,128]{1,0:T(8,128)S(1)}, f32[64,128]{1,0:T(8,128)S(1)}, u32[]{:S(2)}, u32[]{:S(2)}) collective-permute-start(f32[64,128]{1,0:T(8,128)S(1)} %slice.17), channel_id=1, source_target_pairs={{0,4},{4,0},{8,12},{12,8},{16,20},{20,16},{24,28},{28,24},{32,36},... | collective-permute-start | bytes 98312 | tf_op jit(solution)/shard_map/ppermute | solution.py:297
  30.5 0.9 %shard_map.126.refs_1_ = f32[40,2048]{1,0:T(8,128)S(1)} custom-call(f32[40,512]{1,0:T(8,128)S(1)} %get-tuple-element.18.wide_ref.refs_15_, bf16[120,512]{1,0:T(8,128)(2,1)S(1)} %get-tuple-element.23.table_ref, bf16[512,2048]{1,0:T(8,128)(2,1)S(1)} %get-tuple-element.19.own_ref.refs_8_, bf16[768,2048]{1,0:T(8,128)(2,1)S(1)} %get-tuple-element.20.other_ref.refs_9_, ...), custom_call_target="tpu_custom_call" | custom-call | tf_op jit(solution)/shard_map/pallas_call | solution.py:270
  31.6 1.6 %shard_map.128 = (f32[40,512]{1,0:T(8,128)S(1)}, f32[24,512]{1,0:T(8,128)S(1)}, f32[24,128]{1,0:T(8,128)S(1)}, f32[24,128]{1,0:T(8,128)S(1)}) custom-call(s32[1]{0:T(128)S(6)} %copy.13.count_ref.refs_0_, f32[40,2048]{1,0:T(8,128)S(1)} %shard_map.126.refs_1_, f32[24,128]{1,0:T(8,128)S(1)} %collective-permute-done.near_in.refs_2_, ...), custom_call_target="tpu_custom_call" | custom-call | tf_op jit(solution)/shard_map/pallas_call | solution.py:270
  33.4 1.1 %collective-permute-done.8.near_in.refs_2_ = f32[24,128]{1,0:T(8,128)S(1)} collective-permute-done((f32[24,128]{1,0:T(8,128)S(1)}, f32[24,128]{1,0:T(8,128)S(1)}, u32[]{:S(2)}, u32[]{:S(2)}) %collective-permute-start.8) | collective-permute-done | bytes 12320 | tf_op jit(solution)/shard_map/ppermute | solution.py:294
  34.5 3.2 %collective-permute-done.9.cross_in.refs_3_ = f32[48,128]{1,0:T(8,128)S(1)} collective-permute-done((f32[48,128]{1,0:T(8,128)S(1)}, f32[48,128]{1,0:T(8,128)S(1)}, u32[]{:S(2)}, u32[]{:S(2)}) %collective-permute-start.9) | collective-permute-done | bytes 24608 | tf_op jit(solution)/shard_map/ppermute | solution.py:296
  37.8 3.5 %collective-permute-start.10 = (f32[24,128]{1,0:T(8,128)S(1)}, f32[24,128]{1,0:T(8,128)S(1)}, u32[]{:S(2)}, u32[]{:S(2)}) collective-permute-start(f32[24,128]{1,0:T(8,128)S(1)} %slice.18), channel_id=1, source_target_pairs={{0,4},{4,0},{8,12},{12,8},{16,20},{20,16},{24,28},{28,24},{32,36},... | collective-permute-start | bytes 36872 | tf_op jit(solution)/shard_map/ppermute | solution.py:297
  42.1 1.4 %shard_map.130 = (bf16[120,512]{1,0:T(8,128)(2,1)S(1)}, f32[64,128]{1,0:T(8,128)S(1)}, f32[64,128]{1,0:T(8,128)S(1)}) custom-call(s32[1]{0:T(128)S(6)} %copy.13.count_ref.refs_0_, f32[40,2048]{1,0:T(8,128)S(1)} %shard_map.129.jump_ref, f32[24,128]{1,0:T(8,128)S(1)} %collective-permute-done.8.near_in.refs_2_, ...), custom_call_target="tpu_custom_call" | custom-call | tf_op jit(solution)/shard_map/pallas_call | solution.py:270
  44.0 0.6 %collective-permute-start.15 = (f32[48,512]{1,0:T(8,128)S(1)}, f32[48,512]{1,0:T(8,128)S(1)}, u32[]{:S(2)}, u32[]{:S(2)}) collective-permute-start(f32[48,512]{1,0:T(8,128)S(1)} %pad_maximum_fusion.1), channel_id=1, source_target_pairs={{0,3},{1,2},{2,1},{3,0},{4,7},{5,6},{6,5},{7,4},{8,11},{9,10},{10,... | collective-permute-start | bytes 294920 | tf_op jit(solution)/shard_map/ppermute | solution.py:303
  44.9 4.0 %collective-permute-done.12.refs_6_ = f32[128,128]{1,0:T(8,128)S(1)} collective-permute-done((f32[128,128]{1,0:T(8,128)S(1)}, f32[128,128]{1,0:T(8,128)S(1)}, u32[]{:S(2)}, u32[]{:S(2)}) %collective-permute-start.12) | collective-permute-done | bytes 65568 | tf_op jit(solution)/shard_map/ppermute | solution.py:296
  48.9 3.4 %collective-permute-start.13 = (f32[64,128]{1,0:T(8,128)S(1)}, f32[64,128]{1,0:T(8,128)S(1)}, u32[]{:S(2)}, u32[]{:S(2)}) collective-permute-start(f32[64,128]{1,0:T(8,128)S(1)} %slice.19), channel_id=1, source_target_pairs={{0,4},{4,0},{8,12},{12,8},{16,20},{20,16},{24,28},{28,24},{32,36},... | collective-permute-start | bytes 98312 | tf_op jit(solution)/shard_map/ppermute | solution.py:297
  52.3 0.9 %shard_map.131.refs_1_ = f32[40,2048]{1,0:T(8,128)S(1)} custom-call(f32[40,512]{1,0:T(8,128)S(1)} %get-tuple-element.27.wide_ref, bf16[120,512]{1,0:T(8,128)(2,1)S(1)} %get-tuple-element.30.table_ref, bf16[512,2048]{1,0:T(8,128)(2,1)S(1)} %get-tuple-element.19.own_ref.refs_8_, bf16[768,2048]{1,0:T(8,128)(2,1)S(1)} %get-tuple-element.20.other_ref.refs_9_, ...), custom_call_target="tpu_custom_call" | custom-call | tf_op jit(solution)/shard_map/pallas_call | solution.py:270
  53.4 2.1 %shard_map.133 = (f32[5,4,512]{2,1,0:T(4,128)}, f32[5,4,512]{2,1,0:T(4,128)}) custom-call(s32[1]{0:T(128)S(6)} %copy.13.count_ref.refs_0_, f32[40,2048]{1,0:T(8,128)S(1)} %shard_map.131.refs_1_, f32[24,128]{1,0:T(8,128)S(1)} %collective-permute-done.8.near_in.refs_2_, f32[48,128]{1,0:T(8,128)S(1)} %collective-permute-done.9.cross_in.refs_3_, ...), custom_call_target="tpu_custom_call" | custom-call | tf_op jit(solution)/shard_map/pallas_call | solution.py:270
  (54 shorter events, 3.6 us)
Async XLA Ops:
  0.6 18.0 %copy-start = (f32[3,2048]{1,0:T(4,128)S(1)}, f32[3,2048]{1,0:T(4,128)}, u32[]{:S(2)}) copy-start(f32[3,2048]{1,0:T(4,128)} %refs_10_.3) | copy-start | bytes 73732
  2.1 16.5 %copy-start.6 = (f32[512]{0:T(512)S(1)}, f32[512]{0:T(512)}, u32[]{:S(2)}) copy-start(f32[512]{0:T(512)} %param.12) | copy-start | bytes 6148
  2.1 16.5 %copy-start.8 = (s32[4,64]{1,0:T(4,128)S(1)}, s32[4,64]{1,0:T(4,128)}, u32[]{:S(2)}) copy-start(s32[4,64]{1,0:T(4,128)} %send_ref.3) | copy-start | bytes 3076
  2.5 4.1 %collective-permute-start = (f32[24,128]{1,0:T(8,128)S(1)}, f32[24,128]{1,0:T(8,128)S(1)}, u32[]{:S(2)}, u32[]{:S(2)}) collective-permute-start(f32[24,128]{1,0:T(8,128)S(1)} %get-tuple-element.21), channel_id=1, source_target_pairs={{0,4},{4,0},{8,12},{12,8},{16,20},{20,16},{24,28},{28,24},{32,36},... | collective-permute-start | bytes 36872 | tf_op jit(solution)/shard_map/ppermute | solution.py:294
  5.8 14.4 %collective-permute-start.6 = (f32[24,512]{1,0:T(8,128)S(1)}, f32[24,512]{1,0:T(8,128)S(1)}, u32[]{:S(2)}, u32[]{:S(2)}) collective-permute-start(f32[24,512]{1,0:T(8,128)S(1)} %get-tuple-element.26.mine_ref), channel_id=1, source_target_pairs={{0,1},{1,0},{2,3},{3,2},{4,5},{5,4},{6,7},{7,6},{8,9},{9,8},{10,11... | collective-permute-start | bytes 147464 | tf_op jit(solution)/shard_map/ppermute | solution.py:301
  6.6 3.3 %collective-permute-start.1 = (f32[48,128]{1,0:T(8,128)S(1)}, f32[48,128]{1,0:T(8,128)S(1)}, u32[]{:S(2)}, u32[]{:S(2)}) collective-permute-start(f32[48,128]{1,0:T(8,128)S(1)} %pad_maximum_fusion.4), channel_id=1, source_target_pairs={{4,8},{12,16},{20,24},{28,32},{36,40},{44,48},{52,56},{60,64},{68,... | collective-permute-start | bytes 73736 | tf_op jit(solution)/shard_map/ppermute | solution.py:296
  9.8 8.7 %collective-permute-start.2 = (f32[24,128]{1,0:T(8,128)S(1)}, f32[24,128]{1,0:T(8,128)S(1)}, u32[]{:S(2)}, u32[]{:S(2)}) collective-permute-start(f32[24,128]{1,0:T(8,128)S(1)} %slice.16), channel_id=1, source_target_pairs={{0,4},{4,0},{8,12},{12,8},{16,20},{20,16},{24,28},{28,24},{32,36},... | collective-permute-start | bytes 36872 | tf_op jit(solution)/shard_map/ppermute | solution.py:297
  18.6 11.9 %copy-start.1 = (f32[3,2048]{1,0:T(4,128)S(1)}, f32[3,2048]{1,0:T(4,128)}, u32[]{:S(2)}) copy-start(f32[3,2048]{1,0:T(4,128)} %refs_11_.3) | copy-start | bytes 73732
  18.6 11.9 %copy-start.5 = (f32[3,2048]{1,0:T(4,128)S(1)}, f32[3,2048]{1,0:T(4,128)}, u32[]{:S(2)}) copy-start(f32[3,2048]{1,0:T(4,128)} %owner_arm_ref.3) | copy-start | bytes 73732
  20.1 11.4 %copy-start.2 = (f32[4,40,96]{2,1,0:T(8,128)S(1)}, f32[4,40,96]{2,1,0:T(8,128)}, u32[]{:S(2)}) copy-start(f32[4,40,96]{2,1,0:T(8,128)} %constant.2.clone.matrix_ref) | copy-start | bytes 184324
  20.1 2.5 %collective-permute-start.3 = (f32[64,128]{1,0:T(8,128)S(1)}, f32[64,128]{1,0:T(8,128)S(1)}, u32[]{:S(2)}, u32[]{:S(2)}) collective-permute-start(f32[64,128]{1,0:T(8,128)S(1)} %get-tuple-element.24), channel_id=1, source_target_pairs={{0,4},{4,0},{8,12},{12,8},{16,20},{20,16},{24,28},{28,24},{32,36},... | collective-permute-start | bytes 98312 | tf_op jit(solution)/shard_map/ppermute | solution.py:294
  20.2 11.2 %collective-permute-start.7 = (f32[48,512]{1,0:T(8,128)S(1)}, f32[48,512]{1,0:T(8,128)S(1)}, u32[]{:S(2)}, u32[]{:S(2)}) collective-permute-start(f32[48,512]{1,0:T(8,128)S(1)} %pad_maximum_fusion), channel_id=1, source_target_pairs={{0,3},{1,2},{2,1},{3,0},{4,7},{5,6},{6,5},{7,4},{8,11},{9,10},{10,... | collective-permute-start | bytes 294920 | tf_op jit(solution)/shard_map/ppermute | solution.py:303
  22.6 9.1 %copy-start.9 = (f32[512]{0:T(512)S(1)}, f32[512]{0:T(512)}, u32[]{:S(2)}) copy-start(f32[512]{0:T(512)} %param.13) | copy-start | bytes 6148
  22.6 3.8 %collective-permute-start.4 = (f32[128,128]{1,0:T(8,128)S(1)}, f32[128,128]{1,0:T(8,128)S(1)}, u32[]{:S(2)}, u32[]{:S(2)}) collective-permute-start(f32[128,128]{1,0:T(8,128)S(1)} %pad_maximum_fusion.2), channel_id=1, source_target_pairs={{4,8},{12,16},{20,24},{28,32},{36,40},{44,48},{52,56},{60,64},{68,... | collective-permute-start | bytes 196616 | tf_op jit(solution)/shard_map/ppermute | solution.py:296
  26.4 5.2 %collective-permute-start.5 = (f32[64,128]{1,0:T(8,128)S(1)}, f32[64,128]{1,0:T(8,128)S(1)}, u32[]{:S(2)}, u32[]{:S(2)}) collective-permute-start(f32[64,128]{1,0:T(8,128)S(1)} %slice.17), channel_id=1, source_target_pairs={{0,4},{4,0},{8,12},{12,8},{16,20},{20,16},{24,28},{28,24},{32,36},... | collective-permute-start | bytes 98312 | tf_op jit(solution)/shard_map/ppermute | solution.py:297
  33.2 1.3 %collective-permute-start.8 = (f32[24,128]{1,0:T(8,128)S(1)}, f32[24,128]{1,0:T(8,128)S(1)}, u32[]{:S(2)}, u32[]{:S(2)}) collective-permute-start(f32[24,128]{1,0:T(8,128)S(1)} %get-tuple-element.28), channel_id=1, source_target_pairs={{0,4},{4,0},{8,12},{12,8},{16,20},{20,16},{24,28},{28,24},{32,36},... | collective-permute-start | bytes 36872 | tf_op jit(solution)/shard_map/ppermute | solution.py:294
  33.3 10.6 %collective-permute-start.14 = (f32[24,512]{1,0:T(8,128)S(1)}, f32[24,512]{1,0:T(8,128)S(1)}, u32[]{:S(2)}, u32[]{:S(2)}) collective-permute-start(f32[24,512]{1,0:T(8,128)S(1)} %get-tuple-element.33.mine_ref), channel_id=1, source_target_pairs={{0,1},{1,0},{2,3},{3,2},{4,5},{5,4},{6,7},{7,6},{8,9},{9,8},{10,11... | collective-permute-start | bytes 147464 | tf_op jit(solution)/shard_map/ppermute | solution.py:301
  34.5 3.3 %collective-permute-start.9 = (f32[48,128]{1,0:T(8,128)S(1)}, f32[48,128]{1,0:T(8,128)S(1)}, u32[]{:S(2)}, u32[]{:S(2)}) collective-permute-start(f32[48,128]{1,0:T(8,128)S(1)} %pad_maximum_fusion.5), channel_id=1, source_target_pairs={{4,8},{12,16},{20,24},{28,32},{36,40},{44,48},{52,56},{60,64},{68,... | collective-permute-start | bytes 73736 | tf_op jit(solution)/shard_map/ppermute | solution.py:296
  37.8 4.3 %collective-permute-start.10 = (f32[24,128]{1,0:T(8,128)S(1)}, f32[24,128]{1,0:T(8,128)S(1)}, u32[]{:S(2)}, u32[]{:S(2)}) collective-permute-start(f32[24,128]{1,0:T(8,128)S(1)} %slice.18), channel_id=1, source_target_pairs={{0,4},{4,0},{8,12},{12,8},{16,20},{20,16},{24,28},{28,24},{32,36},... | collective-permute-start | bytes 36872 | tf_op jit(solution)/shard_map/ppermute | solution.py:297
  43.5 1.3 %collective-permute-start.11 = (f32[64,128]{1,0:T(8,128)S(1)}, f32[64,128]{1,0:T(8,128)S(1)}, u32[]{:S(2)}, u32[]{:S(2)}) collective-permute-start(f32[64,128]{1,0:T(8,128)S(1)} %get-tuple-element.31), channel_id=1, source_target_pairs={{0,4},{4,0},{8,12},{12,8},{16,20},{20,16},{24,28},{28,24},{32,36},... | collective-permute-start | bytes 98312 | tf_op jit(solution)/shard_map/ppermute | solution.py:294
  44.0 9.2 %collective-permute-start.15 = (f32[48,512]{1,0:T(8,128)S(1)}, f32[48,512]{1,0:T(8,128)S(1)}, u32[]{:S(2)}, u32[]{:S(2)}) collective-permute-start(f32[48,512]{1,0:T(8,128)S(1)} %pad_maximum_fusion.1), channel_id=1, source_target_pairs={{0,3},{1,2},{2,1},{3,0},{4,7},{5,6},{6,5},{7,4},{8,11},{9,10},{10,... | collective-permute-start | bytes 294920 | tf_op jit(solution)/shard_map/ppermute | solution.py:303
  44.8 8.6 %copy-start.4 = (f32[5,4,512]{2,1,0:T(4,128)S(1)}, f32[5,4,512]{2,1,0:T(4,128)}, u32[]{:S(2)}) copy-start(f32[5,4,512]{2,1,0:T(4,128)} %refs_15_.1) | copy-start | bytes 122884
  44.8 4.1 %collective-permute-start.12 = (f32[128,128]{1,0:T(8,128)S(1)}, f32[128,128]{1,0:T(8,128)S(1)}, u32[]{:S(2)}, u32[]{:S(2)}) collective-permute-start(f32[128,128]{1,0:T(8,128)S(1)} %pad_maximum_fusion.3), channel_id=1, source_target_pairs={{4,8},{12,16},{20,24},{28,32},{36,40},{44,48},{52,56},{60,64},{68,... | collective-permute-start | bytes 196616 | tf_op jit(solution)/shard_map/ppermute | solution.py:296
  48.9 4.5 %collective-permute-start.13 = (f32[64,128]{1,0:T(8,128)S(1)}, f32[64,128]{1,0:T(8,128)S(1)}, u32[]{:S(2)}, u32[]{:S(2)}) collective-permute-start(f32[64,128]{1,0:T(8,128)S(1)} %slice.19), channel_id=1, source_target_pairs={{0,4},{4,0},{8,12},{12,8},{16,20},{20,16},{24,28},{28,24},{32,36},... | collective-permute-start | bytes 98312 | tf_op jit(solution)/shard_map/ppermute | solution.py:297
  (4 other events, 2.9 us)

commit v3 on v2

--- a/solution.py
+++ b/solution.py
@@ -98,12 +98,15 @@
 
 
 def send_kernel(
-    state_hbm, send_hbm, near_ref, far_ref, wide_ref, dense_ref, state_ref, send_ref, state_sem, send_sem
+    state_hbm, send_hbm, owner_hbm, neighbor_hbm, near_ref, far_ref, wide_ref, dense_ref, owner_ref, neighbor_ref,
+    state_ref, send_ref, state_sem, send_sem, owner_sem, neighbor_sem,
 ):
+    fetch_send = pltpu.make_async_copy(send_hbm, send_ref, send_sem)
     fetch_state = pltpu.make_async_copy(state_hbm, state_ref, state_sem)
-    fetch_send = pltpu.make_async_copy(send_hbm, send_ref, send_sem)
-    fetch_state.start()
-    fetch_send.start()
+    fetch_owner = pltpu.make_async_copy(owner_hbm, owner_ref, owner_sem)
+    fetch_neighbor = pltpu.make_async_copy(neighbor_hbm, neighbor_ref, neighbor_sem)
+    for fetch in (fetch_send, fetch_state, fetch_owner, fetch_neighbor):
+        fetch.start()
     fetch_send.wait()
     fetch_state.wait()
     for v in range(NV):
@@ -112,6 +115,8 @@
     wide = wide_ref[...]
     write_messages(pieces(wide), send_ref[...], parity_of_partition(), near_ref, far_ref)
     dense_ref[...] = paired([wide[8 * v : 8 * v + 8] for v in range(NV)])
+    fetch_owner.wait()
+    fetch_neighbor.wait()
 
 
 def hot_kernel(owner_ref, neighbor_ref, own_ref, other_ref):
@@ -288,12 +293,17 @@
     neighbor = face_neighbor.reshape(1, FACES)
     matrices = jnp.asarray(spectral_matrices(lax.axis_size("inst"), state.shape[1]))
     inside = [(i, i ^ 1) for i in range(parts)]
-    across = [(i, (i + 1) % parts) for i in range(1, parts, 2)] + [((i + 1) % parts, i) for i in range(1, parts, 2)]
+    lines = lax.axis_size("inst")
+    across = []
+    for i in range(parts):
+        for y in range(lines):
+            j = i + 1 if i % 2 else i - 1
+            across.append((lines * i + y, lines * j + y if 0 <= j < parts else lines * i + (y ^ 1)))
 
     def exchange(near, far):
         got = lax.ppermute(near, "dom", inside)
         outgoing = jnp.concatenate([far, got], axis=0)
-        cross = lax.ppermute(outgoing, "dom", across)
+        cross = lax.ppermute(outgoing, ("dom", "inst"), across)
         relay = lax.ppermute(cross[: far.shape[0]], "dom", inside)
         return got, cross, relay
 
@@ -309,12 +319,11 @@
 
     wide_shape, dense_shape = ((VROWS, CELLS), F32), ((24, CELLS), F32)
     faces_shape = ((VROWS, FACES), F32)
-    near, far, wide, dense = call(
-        send_kernel, message(24) + [wide_shape, dense_shape], [], [state, send_cells], hbm=2,
-        scratch=[
-            pltpu.VMEM(state.shape, F32), pltpu.VMEM(send_cells.shape, jnp.int32), pltpu.SemaphoreType.DMA,
-            pltpu.SemaphoreType.DMA,
-        ],
+    sources = [pltpu.with_memory_space_constraint(x, pltpu.HBM) for x in (state, send_cells, owner, neighbor)]
+    ids = ((1, FACES), jnp.int32)
+    near, far, wide, dense, owner, neighbor = call(
+        send_kernel, message(24) + [wide_shape, dense_shape, ids, ids], [], sources, hbm=4,
+        scratch=[pltpu.VMEM(state.shape, F32), pltpu.VMEM(send_cells.shape, jnp.int32)] + [pltpu.SemaphoreType.DMA] * 4,
     )
     hot = call(hot_kernel, [((CELLS, FACES), BF), ((CELLS + GHOSTS, FACES), BF)], [], [owner, neighbor])
     for section in range(2):

time: 55.7 us -> 50 us (0.90)
  the two profiles are of different devices: /device:TPU:1 before, /device:TPU:129 now
where the time goes in v3:
time: 50 us; the launch traced here: 49.8 us
  starting transfers between devices  22.1 us (44%)
  waiting for transfers between devices  14.3 us (29%)
  Pallas kernels  11.8 us (24%)
  between operations  1.54 us (3%)
    ppermute x4, starting transfers between devices, exchange(): relay = lax.ppermute(cross[:far.shape[0]], 'dom', inside)  14.6 us
    ppermute x4, waiting for transfers between devices, exchange(): cross = lax.ppermute(outgoing, ('dom', 'inst'), across)  12.7 us
    pallas_call x12, Pallas kernels, call(): pl.pallas_call(kernel, out_shape=[jax.ShapeDtypeStruct(s, d) for s, d in...  11.8 us
    ppermute x2, starting transfers between devices, instances(): rest = lax.ppermute(outgoing, 'inst', [(i, i ^ 3) for i in range(4)])  2.96 us
    ppermute x4, starting transfers between devices, exchange(): cross = lax.ppermute(outgoing, ('dom', 'inst'), across)  1.67 us
    ppermute x4, starting transfers between devices, exchange(): got = lax.ppermute(near, 'dom', inside)  1.43 us
    ppermute x2, starting transfers between devices, instances(): one = lax.ppermute(dense, 'inst', [(i, i ^ 1) for i in range(4)])  1.42 us
    ppermute x4, waiting for transfers between devices, exchange(): got = lax.ppermute(near, 'dom', inside)  1.22 us
  transfers between devices with their start and end apart: 16, of which 7 were waited for; matrix products, arithmetic and copies ran while one was open for 0% of the time, Pallas kernels for 14%

profile of v3, /device:TPU:129, one launch (start us, length us, event | category | flops | bytes accessed | tf_op | source)
XLA Modules:
  0.0 49.8 jit_solution(10028944838373287003)
XLA Ops:
  0.7 1.1 %shard_map.122 = (f32[24,128]{1,0:T(8,128)S(1)}, f32[24,128]{1,0:T(8,128)S(1)}, f32[40,512]{1,0:T(8,128)S(1)}, f32[24,512]{1,0:T(8,128)S(1)}, s32[1,2048]{1,0:T(1,128)S(1)}, /*index=5*/s32[1,2048]{1,0:T(1,128)S(1)}) custom-call(f32[5,4,512]{2,1,0:T(4,128)} %refs_15_.1, s32[4,64]{1,0:T(4,128)} %send_ref.3, s32[1,2048]{1,0:T(1,128)} %bitcast.10, ...), custom_call_target="tpu_custom_call" | custom-call | tf_op jit(solution)/shard_map/pallas_call | solution.py:275
  1.8 0.8 %collective-permute-start = (f32[24,128]{1,0:T(8,128)S(1)}, f32[24,128]{1,0:T(8,128)S(1)}, u32[]{:S(2)}, u32[]{:S(2)}) collective-permute-start(f32[24,128]{1,0:T(8,128)S(1)} %get-tuple-element.25), channel_id=1, source_target_pairs={{0,4},{4,0},{8,12},{12,8},{16,20},{20,16},{24,28},{28,24},{32,36},... | collective-permute-start | bytes 36872 | tf_op jit(solution)/shard_map/ppermute | solution.py:304
  2.6 1.3 %collective-permute-start.6 = (f32[24,512]{1,0:T(8,128)S(1)}, f32[24,512]{1,0:T(8,128)S(1)}, u32[]{:S(2)}, u32[]{:S(2)}) collective-permute-start(f32[24,512]{1,0:T(8,128)S(1)} %get-tuple-element.30.mine_ref), channel_id=1, source_target_pairs={{0,1},{1,0},{2,3},{3,2},{4,5},{5,4},{6,7},{7,6},{8,9},{9,8},{10,11... | collective-permute-start | bytes 147464 | tf_op jit(solution)/shard_map/ppermute | solution.py:311
  3.9 1.5 %collective-permute-start.1 = (f32[48,128]{1,0:T(8,128)S(1)}, f32[48,128]{1,0:T(8,128)S(1)}, u32[]{:S(2)}, u32[]{:S(2)}) collective-permute-start(f32[48,128]{1,0:T(8,128)S(1)} %pad_maximum_fusion.4), channel_id=1, source_target_pairs={{0,1},{1,0},{2,3},{3,2},{4,8},{5,9},{6,10},{7,11},{8,4},{9,5},{10,... | collective-permute-start | bytes 73736 | tf_op jit(solution)/shard_map/ppermute | solution.py:306
  5.4 1.8 %collective-permute-done.1.cross_in.refs_3_ = f32[48,128]{1,0:T(8,128)S(1)} collective-permute-done((f32[48,128]{1,0:T(8,128)S(1)}, f32[48,128]{1,0:T(8,128)S(1)}, u32[]{:S(2)}, u32[]{:S(2)}) %collective-permute-start.1) | collective-permute-done | bytes 24608 | tf_op jit(solution)/shard_map/ppermute | solution.py:306
  7.1 3.7 %collective-permute-start.2 = (f32[24,128]{1,0:T(8,128)S(1)}, f32[24,128]{1,0:T(8,128)S(1)}, u32[]{:S(2)}, u32[]{:S(2)}) collective-permute-start(f32[24,128]{1,0:T(8,128)S(1)} %slice.16), channel_id=1, source_target_pairs={{0,4},{4,0},{8,12},{12,8},{16,20},{20,16},{24,28},{28,24},{32,36},... | collective-permute-start | bytes 36872 | tf_op jit(solution)/shard_map/ppermute | solution.py:307
  11.5 1.0 %shard_map.123 = (bf16[512,2048]{1,0:T(8,128)(2,1)S(1)}, bf16[768,2048]{1,0:T(8,128)(2,1)S(1)}) custom-call(s32[1,2048]{1,0:T(1,128)S(1)} %get-tuple-element.21.owner_ref, s32[1,2048]{1,0:T(1,128)S(1)} %get-tuple-element.22.neighbor_ref), custom_call_target="tpu_custom_call" | custom-call | tf_op jit(solution)/shard_map/pallas_call | solution.py:275
  12.5 0.5 shard_map.124.jump_ref
  13.0 1.4 %shard_map.125 = (bf16[120,512]{1,0:T(8,128)(2,1)S(1)}, f32[64,128]{1,0:T(8,128)S(1)}, f32[64,128]{1,0:T(8,128)S(1)}) custom-call(s32[1]{0:T(128)S(6)} %copy.13.count_ref.refs_0_, f32[40,2048]{1,0:T(8,128)S(1)} %shard_map.124.jump_ref, f32[24,128]{1,0:T(8,128)S(1)} %collective-permute-done.near_in.refs_2_, ...), custom_call_target="tpu_custom_call" | custom-call | tf_op jit(solution)/shard_map/pallas_call | solution.py:275
  14.6 2.3 %collective-permute-start.7 = (f32[48,512]{1,0:T(8,128)S(1)}, f32[48,512]{1,0:T(8,128)S(1)}, u32[]{:S(2)}, u32[]{:S(2)}) collective-permute-start(f32[48,512]{1,0:T(8,128)S(1)} %pad_maximum_fusion), channel_id=1, source_target_pairs={{0,3},{1,2},{2,1},{3,0},{4,7},{5,6},{6,5},{7,4},{8,11},{9,10},{10,... | collective-permute-start | bytes 294920 | tf_op jit(solution)/shard_map/ppermute | solution.py:313
  17.1 3.7 %collective-permute-done.4.refs_6_ = f32[128,128]{1,0:T(8,128)S(1)} collective-permute-done((f32[128,128]{1,0:T(8,128)S(1)}, f32[128,128]{1,0:T(8,128)S(1)}, u32[]{:S(2)}, u32[]{:S(2)}) %collective-permute-start.4) | collective-permute-done | bytes 65568 | tf_op jit(solution)/shard_map/ppermute | solution.py:306
  20.7 4.1 %collective-permute-start.5 = (f32[64,128]{1,0:T(8,128)S(1)}, f32[64,128]{1,0:T(8,128)S(1)}, u32[]{:S(2)}, u32[]{:S(2)}) collective-permute-start(f32[64,128]{1,0:T(8,128)S(1)} %slice.17), channel_id=1, source_target_pairs={{0,4},{4,0},{8,12},{12,8},{16,20},{20,16},{24,28},{28,24},{32,36},... | collective-permute-start | bytes 98312 | tf_op jit(solution)/shard_map/ppermute | solution.py:307
  24.8 0.9 %shard_map.126.refs_1_ = f32[40,2048]{1,0:T(8,128)S(1)} custom-call(f32[40,512]{1,0:T(8,128)S(1)} %get-tuple-element.20.wide_ref.refs_15_, bf16[120,512]{1,0:T(8,128)(2,1)S(1)} %get-tuple-element.27.table_ref, bf16[512,2048]{1,0:T(8,128)(2,1)S(1)} %get-tuple-element.23.own_ref.refs_8_, bf16[768,2048]{1,0:T(8,128)(2,1)S(1)} %get-tuple-element.24.other_ref.refs_9_, ...), custom_call_target="tpu_custom_call" | custom-call | tf_op jit(solution)/shard_map/pallas_call | solution.py:275
  26.0 1.6 %shard_map.128 = (f32[40,512]{1,0:T(8,128)S(1)}, f32[24,512]{1,0:T(8,128)S(1)}, f32[24,128]{1,0:T(8,128)S(1)}, f32[24,128]{1,0:T(8,128)S(1)}) custom-call(s32[1]{0:T(128)S(6)} %copy.13.count_ref.refs_0_, f32[40,2048]{1,0:T(8,128)S(1)} %shard_map.126.refs_1_, f32[24,128]{1,0:T(8,128)S(1)} %collective-permute-done.near_in.refs_2_, ...), custom_call_target="tpu_custom_call" | custom-call | tf_op jit(solution)/shard_map/pallas_call | solution.py:275
  27.8 1.0 %collective-permute-done.8.near_in.refs_2_ = f32[24,128]{1,0:T(8,128)S(1)} collective-permute-done((f32[24,128]{1,0:T(8,128)S(1)}, f32[24,128]{1,0:T(8,128)S(1)}, u32[]{:S(2)}, u32[]{:S(2)}) %collective-permute-start.8) | collective-permute-done | bytes 12320 | tf_op jit(solution)/shard_map/ppermute | solution.py:304
  28.8 3.2 %collective-permute-done.9.cross_in.refs_3_ = f32[48,128]{1,0:T(8,128)S(1)} collective-permute-done((f32[48,128]{1,0:T(8,128)S(1)}, f32[48,128]{1,0:T(8,128)S(1)}, u32[]{:S(2)}, u32[]{:S(2)}) %collective-permute-start.9) | collective-permute-done | bytes 24608 | tf_op jit(solution)/shard_map/ppermute | solution.py:306
  32.1 3.5 %collective-permute-start.10 = (f32[24,128]{1,0:T(8,128)S(1)}, f32[24,128]{1,0:T(8,128)S(1)}, u32[]{:S(2)}, u32[]{:S(2)}) collective-permute-start(f32[24,128]{1,0:T(8,128)S(1)} %slice.18), channel_id=1, source_target_pairs={{0,4},{4,0},{8,12},{12,8},{16,20},{20,16},{24,28},{28,24},{32,36},... | collective-permute-start | bytes 36872 | tf_op jit(solution)/shard_map/ppermute | solution.py:307
  35.6 0.5 shard_map.129.jump_ref
  36.4 1.4 %shard_map.130 = (bf16[120,512]{1,0:T(8,128)(2,1)S(1)}, f32[64,128]{1,0:T(8,128)S(1)}, f32[64,128]{1,0:T(8,128)S(1)}) custom-call(s32[1]{0:T(128)S(6)} %copy.13.count_ref.refs_0_, f32[40,2048]{1,0:T(8,128)S(1)} %shard_map.129.jump_ref, f32[24,128]{1,0:T(8,128)S(1)} %collective-permute-done.8.near_in.refs_2_, ...), custom_call_target="tpu_custom_call" | custom-call | tf_op jit(solution)/shard_map/pallas_call | solution.py:275
  38.3 0.6 %collective-permute-start.15 = (f32[48,512]{1,0:T(8,128)S(1)}, f32[48,512]{1,0:T(8,128)S(1)}, u32[]{:S(2)}, u32[]{:S(2)}) collective-permute-start(f32[48,512]{1,0:T(8,128)S(1)} %pad_maximum_fusion.1), channel_id=1, source_target_pairs={{0,3},{1,2},{2,1},{3,0},{4,7},{5,6},{6,5},{7,4},{8,11},{9,10},{10,... | collective-permute-start | bytes 294920 | tf_op jit(solution)/shard_map/ppermute | solution.py:313
  39.3 4.0 %collective-permute-done.12.refs_6_ = f32[128,128]{1,0:T(8,128)S(1)} collective-permute-done((f32[128,128]{1,0:T(8,128)S(1)}, f32[128,128]{1,0:T(8,128)S(1)}, u32[]{:S(2)}, u32[]{:S(2)}) %collective-permute-start.12) | collective-permute-done | bytes 65568 | tf_op jit(solution)/shard_map/ppermute | solution.py:306
  43.2 3.4 %collective-permute-start.13 = (f32[64,128]{1,0:T(8,128)S(1)}, f32[64,128]{1,0:T(8,128)S(1)}, u32[]{:S(2)}, u32[]{:S(2)}) collective-permute-start(f32[64,128]{1,0:T(8,128)S(1)} %slice.19), channel_id=1, source_target_pairs={{0,4},{4,0},{8,12},{12,8},{16,20},{20,16},{24,28},{28,24},{32,36},... | collective-permute-start | bytes 98312 | tf_op jit(solution)/shard_map/ppermute | solution.py:307
  46.6 0.9 %shard_map.131.refs_1_ = f32[40,2048]{1,0:T(8,128)S(1)} custom-call(f32[40,512]{1,0:T(8,128)S(1)} %get-tuple-element.31.wide_ref, bf16[120,512]{1,0:T(8,128)(2,1)S(1)} %get-tuple-element.34.table_ref, bf16[512,2048]{1,0:T(8,128)(2,1)S(1)} %get-tuple-element.23.own_ref.refs_8_, bf16[768,2048]{1,0:T(8,128)(2,1)S(1)} %get-tuple-element.24.other_ref.refs_9_, ...), custom_call_target="tpu_custom_call" | custom-call | tf_op jit(solution)/shard_map/pallas_call | solution.py:275
  47.8 2.1 %shard_map.133 = (f32[5,4,512]{2,1,0:T(4,128)}, f32[5,4,512]{2,1,0:T(4,128)}) custom-call(s32[1]{0:T(128)S(6)} %copy.13.count_ref.refs_0_, f32[40,2048]{1,0:T(8,128)S(1)} %shard_map.131.refs_1_, f32[24,128]{1,0:T(8,128)S(1)} %collective-permute-done.8.near_in.refs_2_, f32[48,128]{1,0:T(8,128)S(1)} %collective-permute-done.9.cross_in.refs_3_, ...), custom_call_target="tpu_custom_call" | custom-call | tf_op jit(solution)/shard_map/pallas_call | solution.py:275
  (46 shorter events, 2.0 us)
Async XLA Ops:
  0.6 12.4 %copy-start.6 = (s32[4,64]{1,0:T(4,128)S(1)}, s32[4,64]{1,0:T(4,128)}, u32[]{:S(2)}) copy-start(s32[4,64]{1,0:T(4,128)} %send_ref.3) | copy-start | bytes 3076
  0.6 12.4 %copy-start = (f32[3,2048]{1,0:T(4,128)S(1)}, f32[3,2048]{1,0:T(4,128)}, u32[]{:S(2)}) copy-start(f32[3,2048]{1,0:T(4,128)} %refs_10_.3) | copy-start | bytes 73732
  0.7 12.4 %copy-start.5 = (f32[512]{0:T(512)S(1)}, f32[512]{0:T(512)}, u32[]{:S(2)}) copy-start(f32[512]{0:T(512)} %param.12) | copy-start | bytes 6148
  1.8 2.1 %collective-permute-start = (f32[24,128]{1,0:T(8,128)S(1)}, f32[24,128]{1,0:T(8,128)S(1)}, u32[]{:S(2)}, u32[]{:S(2)}) collective-permute-start(f32[24,128]{1,0:T(8,128)S(1)} %get-tuple-element.25), channel_id=1, source_target_pairs={{0,4},{4,0},{8,12},{12,8},{16,20},{20,16},{24,28},{28,24},{32,36},... | collective-permute-start | bytes 36872 | tf_op jit(solution)/shard_map/ppermute | solution.py:304
  2.6 12.0 %collective-permute-start.6 = (f32[24,512]{1,0:T(8,128)S(1)}, f32[24,512]{1,0:T(8,128)S(1)}, u32[]{:S(2)}, u32[]{:S(2)}) collective-permute-start(f32[24,512]{1,0:T(8,128)S(1)} %get-tuple-element.30.mine_ref), channel_id=1, source_target_pairs={{0,1},{1,0},{2,3},{3,2},{4,5},{5,4},{6,7},{7,6},{8,9},{9,8},{10,11... | collective-permute-start | bytes 147464 | tf_op jit(solution)/shard_map/ppermute | solution.py:311
  3.9 3.3 %collective-permute-start.1 = (f32[48,128]{1,0:T(8,128)S(1)}, f32[48,128]{1,0:T(8,128)S(1)}, u32[]{:S(2)}, u32[]{:S(2)}) collective-permute-start(f32[48,128]{1,0:T(8,128)S(1)} %pad_maximum_fusion.4), channel_id=1, source_target_pairs={{0,1},{1,0},{2,3},{3,2},{4,8},{5,9},{6,10},{7,11},{8,4},{9,5},{10,... | collective-permute-start | bytes 73736 | tf_op jit(solution)/shard_map/ppermute | solution.py:306
  7.1 5.9 %collective-permute-start.2 = (f32[24,128]{1,0:T(8,128)S(1)}, f32[24,128]{1,0:T(8,128)S(1)}, u32[]{:S(2)}, u32[]{:S(2)}) collective-permute-start(f32[24,128]{1,0:T(8,128)S(1)} %slice.16), channel_id=1, source_target_pairs={{0,4},{4,0},{8,12},{12,8},{16,20},{20,16},{24,28},{28,24},{32,36},... | collective-permute-start | bytes 36872 | tf_op jit(solution)/shard_map/ppermute | solution.py:307
  13.0 11.9 %copy-start.1 = (f32[3,2048]{1,0:T(4,128)S(1)}, f32[3,2048]{1,0:T(4,128)}, u32[]{:S(2)}) copy-start(f32[3,2048]{1,0:T(4,128)} %refs_11_.3) | copy-start | bytes 73732
  13.0 11.8 %copy-start.4 = (f32[3,2048]{1,0:T(4,128)S(1)}, f32[3,2048]{1,0:T(4,128)}, u32[]{:S(2)}) copy-start(f32[3,2048]{1,0:T(4,128)} %owner_arm_ref.3) | copy-start | bytes 73732
  14.5 11.3 %copy-start.2 = (f32[4,40,96]{2,1,0:T(8,128)S(1)}, f32[4,40,96]{2,1,0:T(8,128)}, u32[]{:S(2)}) copy-start(f32[4,40,96]{2,1,0:T(8,128)} %constant.2.clone.matrix_ref) | copy-start | bytes 184324
  14.5 2.5 %collective-permute-start.3 = (f32[64,128]{1,0:T(8,128)S(1)}, f32[64,128]{1,0:T(8,128)S(1)}, u32[]{:S(2)}, u32[]{:S(2)}) collective-permute-start(f32[64,128]{1,0:T(8,128)S(1)} %get-tuple-element.28), channel_id=1, source_target_pairs={{0,4},{4,0},{8,12},{12,8},{16,20},{20,16},{24,28},{28,24},{32,36},... | collective-permute-start | bytes 98312 | tf_op jit(solution)/shard_map/ppermute | solution.py:304
  14.6 11.1 %collective-permute-start.7 = (f32[48,512]{1,0:T(8,128)S(1)}, f32[48,512]{1,0:T(8,128)S(1)}, u32[]{:S(2)}, u32[]{:S(2)}) collective-permute-start(f32[48,512]{1,0:T(8,128)S(1)} %pad_maximum_fusion), channel_id=1, source_target_pairs={{0,3},{1,2},{2,1},{3,0},{4,7},{5,6},{6,5},{7,4},{8,11},{9,10},{10,... | collective-permute-start | bytes 294920 | tf_op jit(solution)/shard_map/ppermute | solution.py:313
  16.9 9.0 %copy-start.7 = (f32[512]{0:T(512)S(1)}, f32[512]{0:T(512)}, u32[]{:S(2)}) copy-start(f32[512]{0:T(512)} %param.13) | copy-start | bytes 6148
  17.0 3.8 %collective-permute-start.4 = (f32[128,128]{1,0:T(8,128)S(1)}, f32[128,128]{1,0:T(8,128)S(1)}, u32[]{:S(2)}, u32[]{:S(2)}) collective-permute-start(f32[128,128]{1,0:T(8,128)S(1)} %pad_maximum_fusion.2), channel_id=1, source_target_pairs={{0,1},{1,0},{2,3},{3,2},{4,8},{5,9},{6,10},{7,11},{8,4},{9,5},{10,... | collective-permute-start | bytes 196616 | tf_op jit(solution)/shard_map/ppermute | solution.py:306
  20.7 5.2 %collective-permute-start.5 = (f32[64,128]{1,0:T(8,128)S(1)}, f32[64,128]{1,0:T(8,128)S(1)}, u32[]{:S(2)}, u32[]{:S(2)}) collective-permute-start(f32[64,128]{1,0:T(8,128)S(1)} %slice.17), channel_id=1, source_target_pairs={{0,4},{4,0},{8,12},{12,8},{16,20},{20,16},{24,28},{28,24},{32,36},... | collective-permute-start | bytes 98312 | tf_op jit(solution)/shard_map/ppermute | solution.py:307
  27.6 1.3 %collective-permute-start.8 = (f32[24,128]{1,0:T(8,128)S(1)}, f32[24,128]{1,0:T(8,128)S(1)}, u32[]{:S(2)}, u32[]{:S(2)}) collective-permute-start(f32[24,128]{1,0:T(8,128)S(1)} %get-tuple-element.32), channel_id=1, source_target_pairs={{0,4},{4,0},{8,12},{12,8},{16,20},{20,16},{24,28},{28,24},{32,36},... | collective-permute-start | bytes 36872 | tf_op jit(solution)/shard_map/ppermute | solution.py:304
  27.7 10.6 %collective-permute-start.14 = (f32[24,512]{1,0:T(8,128)S(1)}, f32[24,512]{1,0:T(8,128)S(1)}, u32[]{:S(2)}, u32[]{:S(2)}) collective-permute-start(f32[24,512]{1,0:T(8,128)S(1)} %get-tuple-element.37.mine_ref), channel_id=1, source_target_pairs={{0,1},{1,0},{2,3},{3,2},{4,5},{5,4},{6,7},{7,6},{8,9},{9,8},{10,11... | collective-permute-start | bytes 147464 | tf_op jit(solution)/shard_map/ppermute | solution.py:311
  28.8 3.3 %collective-permute-start.9 = (f32[48,128]{1,0:T(8,128)S(1)}, f32[48,128]{1,0:T(8,128)S(1)}, u32[]{:S(2)}, u32[]{:S(2)}) collective-permute-start(f32[48,128]{1,0:T(8,128)S(1)} %pad_maximum_fusion.5), channel_id=1, source_target_pairs={{0,1},{1,0},{2,3},{3,2},{4,8},{5,9},{6,10},{7,11},{8,4},{9,5},{10,... | collective-permute-start | bytes 73736 | tf_op jit(solution)/shard_map/ppermute | solution.py:306
  32.1 4.3 %collective-permute-start.10 = (f32[24,128]{1,0:T(8,128)S(1)}, f32[24,128]{1,0:T(8,128)S(1)}, u32[]{:S(2)}, u32[]{:S(2)}) collective-permute-start(f32[24,128]{1,0:T(8,128)S(1)} %slice.18), channel_id=1, source_target_pairs={{0,4},{4,0},{8,12},{12,8},{16,20},{20,16},{24,28},{28,24},{32,36},... | collective-permute-start | bytes 36872 | tf_op jit(solution)/shard_map/ppermute | solution.py:307
  37.9 1.3 %collective-permute-start.11 = (f32[64,128]{1,0:T(8,128)S(1)}, f32[64,128]{1,0:T(8,128)S(1)}, u32[]{:S(2)}, u32[]{:S(2)}) collective-permute-start(f32[64,128]{1,0:T(8,128)S(1)} %get-tuple-element.35), channel_id=1, source_target_pairs={{0,4},{4,0},{8,12},{12,8},{16,20},{20,16},{24,28},{28,24},{32,36},... | collective-permute-start | bytes 98312 | tf_op jit(solution)/shard_map/ppermute | solution.py:304
  38.3 9.2 %collective-permute-start.15 = (f32[48,512]{1,0:T(8,128)S(1)}, f32[48,512]{1,0:T(8,128)S(1)}, u32[]{:S(2)}, u32[]{:S(2)}) collective-permute-start(f32[48,512]{1,0:T(8,128)S(1)} %pad_maximum_fusion.1), channel_id=1, source_target_pairs={{0,3},{1,2},{2,1},{3,0},{4,7},{5,6},{6,5},{7,4},{8,11},{9,10},{10,... | collective-permute-start | bytes 294920 | tf_op jit(solution)/shard_map/ppermute | solution.py:313
  39.2 8.6 %copy-start.3 = (f32[5,4,512]{2,1,0:T(4,128)S(1)}, f32[5,4,512]{2,1,0:T(4,128)}, u32[]{:S(2)}) copy-start(f32[5,4,512]{2,1,0:T(4,128)} %refs_15_.1) | copy-start | bytes 122884
  39.2 4.1 %collective-permute-start.12 = (f32[128,128]{1,0:T(8,128)S(1)}, f32[128,128]{1,0:T(8,128)S(1)}, u32[]{:S(2)}, u32[]{:S(2)}) collective-permute-start(f32[128,128]{1,0:T(8,128)S(1)} %pad_maximum_fusion.3), channel_id=1, source_target_pairs={{0,1},{1,0},{2,3},{3,2},{4,8},{5,9},{6,10},{7,11},{8,4},{9,5},{10,... | collective-permute-start | bytes 196616 | tf_op jit(solution)/shard_map/ppermute | solution.py:306
  43.2 4.5 %collective-permute-start.13 = (f32[64,128]{1,0:T(8,128)S(1)}, f32[64,128]{1,0:T(8,128)S(1)}, u32[]{:S(2)}, u32[]{:S(2)}) collective-permute-start(f32[64,128]{1,0:T(8,128)S(1)} %slice.19), channel_id=1, source_target_pairs={{0,4},{4,0},{8,12},{12,8},{16,20},{20,16},{24,28},{28,24},{32,36},... | collective-permute-start | bytes 98312 | tf_op jit(solution)/shard_map/ppermute | solution.py:307

commit v4 on v3

v4 whole, which is shorter than its diff:
```python
import jax
import jax.numpy as jnp
import numpy as np
from jax import lax
from jax.experimental import pallas as pl
from jax.experimental.pallas import tpu as pltpu
from jax.sharding import PartitionSpec as P


HEAT_RATIO = 1.4
FREQUENCY = 0.5
NV = 5
CELLS = 512
GHOSTS = 256
FACES = 2048
CHUNK = 512
VROWS = 24
GROWS = 64
BF = jnp.bfloat16
F32 = jnp.float32


def parity_of_partition():
    return lax.axis_index("dom") & 1


def top_rows(shape):
    return (lax.broadcasted_iota(jnp.int32, shape, 0) & 7) < 4


def swap_halves(x):
    return pltpu.roll(x, 4, 0)


def fold(x):
    return x + swap_halves(x)


def split(x):
    high = x.astype(BF).astype(F32)
    return jnp.concatenate([high, x - high], axis=0).astype(BF)


def joined(x):
    rows = x.shape[0] // 2
    return x[:rows] + x[rows:]


def matmul(a, b):
    return jnp.dot(a, b, preferred_element_type=F32)


def matmul_t(a, b):
    return lax.dot_general(a, b, (((1,), (1,)), ((), ())), preferred_element_type=F32)


def one_hot(ids, rows):
    cell = lax.broadcasted_iota(jnp.int32, (rows, ids.shape[1]), 0)
    return jnp.where(cell == ids, 1.0, 0.0)


def low_lanes(shape):
    return lax.broadcasted_iota(jnp.int32, shape, 1) < 64


def listed(table, send_hot):
    packed = joined(matmul(table, send_hot))
    up, down = packed[:, :128], packed[:, 128:]
    even = parity_of_partition() == 0
    return jnp.where(even, up, down), jnp.where(even, down, up)


def dense_lists(near):
    half = near.shape[0] // 2
    turned = pltpu.roll(near[half:], 64, 1)
    low = low_lanes(turned.shape)
    first, second = jnp.where(low, near[:half], turned), jnp.where(low, turned, near[:half])
    even = parity_of_partition() == 0
    return jnp.concatenate([jnp.where(even, first, second), jnp.where(even, second, first)], axis=0)


def loose(x):
    return jnp.concatenate([x, pltpu.roll(x, 64, 1)], axis=0)


def ghost_values(near, first, second, relay):
    low = low_lanes(near.shape)
    even = parity_of_partition() == 0
    left = jnp.where(low, jnp.where(even, second, relay), jnp.where(even, first, near))
    right = jnp.where(low, jnp.where(even, near, first), jnp.where(even, relay, second))
    return split(jnp.concatenate([left, right], axis=1))


def state_ghosts(near_in, cross_in, relay_in):
    return ghost_values(near_in[...], cross_in[:VROWS], cross_in[VROWS:], relay_in[...])


def gradient_ghosts(near_in, cross_in, relay_in):
    half = GROWS // 2
    return ghost_values(loose(near_in[half:]), cross_in[:GROWS], loose(cross_in[GROWS:]), relay_in[...])


def send_kernel(
    state_hbm, send_hbm, owner_hbm, neighbor_hbm, near_ref, far_ref, dense_ref, hot_ref, owner_ref, neighbor_ref,
    state_ref, send_ref, state_sem, send_sem, owner_sem, neighbor_sem,
):
    fetch_send = pltpu.make_async_copy(send_hbm, send_ref, send_sem)
    fetch_state = pltpu.make_async_copy(state_hbm, state_ref, state_sem)
    fetch_owner = pltpu.make_async_copy(owner_hbm, owner_ref, owner_sem)
    fetch_neighbor = pltpu.make_async_copy(neighbor_hbm, neighbor_ref, neighbor_sem)
    for fetch in (fetch_send, fetch_state, fetch_owner, fetch_neighbor):
        fetch.start()
    fetch_send.wait()
    for k in range(0, 4, 2):
        pair = [one_hot(send_ref[k + j : k + j + 1, :], CELLS) for j in range(2)]
        hot_ref[:, 64 * k : 64 * k + 128] = jnp.concatenate(pair, axis=1).astype(BF)
    fetch_state.wait()
    for v in range(NV):
        dense_ref[4 * v : 4 * v + 4, :] = state_ref[v]
    dense_ref[4 * NV : VROWS, :] = state_ref[NV - 1]
    near_ref[...], far_ref[...] = listed(split(dense_ref[...]), hot_ref[...])
    fetch_owner.wait()
    fetch_neighbor.wait()


def hot_kernel(owner_ref, neighbor_ref, own_ref, other_ref):
    for f in range(0, FACES, CHUNK):
        faces = slice(f, f + CHUNK)
        own_ref[:, faces] = one_hot(owner_ref[:, faces], CELLS).astype(BF)
        other_ref[:, faces] = one_hot(neighbor_ref[:, faces], CELLS + GHOSTS).astype(BF)


def jump_kernel(dense_ref, own_ref, other_ref, jump_ref):
    values = split(dense_ref[...])
    for f in range(0, FACES, CHUNK):
        faces = slice(f, f + CHUNK)
        jump_ref[:, faces] = joined(matmul(values, other_ref[:CELLS, faces] - own_ref[:, faces]))


def gradient_kernel(
    count_ref, jump_ref, near_in, cross_in, relay_in, own_ref, other_ref, normal_ref, volume_ref, send_ref,
    table_ref, near_ref, far_ref,
):
    ghosts = state_ghosts(near_in, cross_in, relay_in)
    total = jnp.zeros((2 * GROWS, CELLS), F32)
    top = top_rows((8, CHUNK))
    for f in range(0, FACES, CHUNK):
        faces = slice(f, f + CHUNK)
        jump = jump_ref[:, faces] + joined(matmul(ghosts, other_ref[CELLS:, faces]))
        live = lax.broadcasted_iota(jnp.int32, (1, CHUNK), 1) + f < count_ref[0]
        half = [jnp.where(live, 0.5 * normal_ref[d : d + 1, faces], 0.0) for d in range(3)]
        flows = [jump[8 * j : 8 * j + 8] * half[d] for d in range(3) for j in range(2)]
        flows += [jump[16:24] * jnp.where(top, half[0], half[1]), jump[16:24] * half[2]]
        sum_hot = other_ref[:CELLS, faces] + own_ref[:, faces]
        total = total + matmul_t(split(jnp.concatenate(flows, axis=0)), sum_hot)
    table = split(joined(total) * (1.0 / volume_ref[...]))
    table_ref[...] = table
    near, far_ref[...] = listed(table, send_ref[...])
    near_ref[...] = dense_lists(near)


def with_arms(values, arm_ref, faces, top):
    state = joined(values[: 2 * VROWS])
    gradient = joined(values[2 * VROWS :])
    arms = [arm_ref[d : d + 1, faces] for d in range(3)]
    out = []
    for j in range(2):
        total = state[8 * j : 8 * j + 8]
        for d in range(3):
            total = total + gradient[16 * d + 8 * j : 16 * d + 8 * j + 8] * arms[d]
        out.append(total)
    energy = fold(gradient[48:56] * jnp.where(top, arms[0], arms[1])) + gradient[56:64] * arms[2]
    out.append(state[16:24] + energy)
    return out


def face_kernel(dense_ref, table_ref, own_ref, other_ref, owner_arm_ref, neighbor_arm_ref, face_ref):
    values = jnp.concatenate([split(dense_ref[...]), table_ref[...]], axis=0)
    top = top_rows((8, CHUNK))
    for f in range(0, FACES, CHUNK):
        faces = slice(f, f + CHUNK)
        left = with_arms(matmul(values, own_ref[:, faces]), owner_arm_ref, faces, top)
        right = with_arms(matmul(values, other_ref[:CELLS, faces]), neighbor_arm_ref, faces, top)
        for j in range(2):
            face_ref[16 * j : 16 * j + 8, faces] = jnp.where(top, left[j], swap_halves(right[j]))
            face_ref[16 * j + 8 : 16 * j + 16, faces] = jnp.where(top, swap_halves(left[j]), right[j])
        face_ref[32:40, faces] = jnp.where(top, left[2], right[2])


def spatial_part(
    count_ref, face_ref, near_in, cross_in, relay_in, gnear_in, gcross_in, grelay_in, own_ref, other_ref, normal_ref,
    neighbor_arm_ref, volume_ref,
):
    ghosts = state_ghosts(near_in, cross_in, relay_in)
    values = jnp.concatenate([ghosts, gradient_ghosts(gnear_in, gcross_in, grelay_in)], axis=0)
    total = jnp.zeros((2 * VROWS, CELLS), F32)
    top = top_rows((8, CHUNK))
    sign = jnp.where(top, 1.0, -1.0)
    for f in range(0, FACES, CHUNK):
        faces = slice(f, f + CHUNK)
        right = with_arms(matmul(values, other_ref[CELLS:, faces]), neighbor_arm_ref, faces, top)
        bottom = [swap_halves(right[0]), right[0], swap_halves(right[1]), right[1], right[2]]
        states = [face_ref[8 * v : 8 * v + 8, faces] + jnp.where(top, 0.0, bottom[v]) for v in range(NV)]
        live = lax.broadcasted_iota(jnp.int32, (1, CHUNK), 1) + f < count_ref[0]
        normals = [jnp.where(live, normal_ref[d : d + 1, faces], 0.0) for d in range(3)]
        area = jnp.sqrt(normals[0] * normals[0] + normals[1] * normals[1] + normals[2] * normals[2])
        density, energy = states[0], states[4]
        momentum = states[1:4]
        inverse = 1.0 / density
        velocity = [m * inverse for m in momentum]
        kinetic = momentum[0] * velocity[0] + momentum[1] * velocity[1] + momentum[2] * velocity[2]
        pressure = (HEAT_RATIO - 1.0) * (energy - 0.5 * kinetic)
        speed = velocity[0] * normals[0] + velocity[1] * normals[1] + velocity[2] * normals[2]
        wave = jnp.abs(speed) + jnp.sqrt(HEAT_RATIO * pressure * inverse) * area
        wave = jnp.maximum(wave, swap_halves(wave)) * sign
        flux = [density * speed]
        for d in range(3):
            flux.append(momentum[d] * speed + pressure * normals[d])
        flux.append((energy + pressure) * speed)
        twice = [flux[v] + wave * states[v] for v in range(NV)]
        sums = []
        for j in range(2):
            a, b = twice[2 * j], twice[2 * j + 1]
            sums.append(jnp.where(top, a, b) + swap_halves(jnp.where(top, b, a)))
        sums.append(fold(twice[4]))
        difference = own_ref[:, faces] - other_ref[:CELLS, faces]
        total = total + matmul_t(split(jnp.concatenate(sums, axis=0)), difference)
    return joined(total) * (0.5 / volume_ref[...])


def middle_kernel(*refs):
    *common, spectral_ref, step_ref, dense_ref, send_ref, dense_out, near_ref, far_ref = refs
    rate = spatial_part(*common) + spectral_ref[...]
    dense = dense_ref[...] - 0.5 * step_ref[...] * rate
    dense_out[...] = dense
    near_ref[...], far_ref[...] = listed(split(dense), send_ref[...])


def last_kernel(*refs):
    *common, spectral_ref, step_ref, state_ref, new_ref, residual_ref = refs
    rate = spatial_part(*common) + spectral_ref[...]
    for v in range(NV):
        rows = rate[4 * v : 4 * v + 4]
        residual_ref[v] = rows
        new_ref[v] = state_ref[v] - step_ref[...] * rows


def spectral_kernel(matrix_ref, mine_ref, next_ref, rest_ref, out_ref):
    matrix = matrix_ref[lax.axis_index("inst")]
    data = jnp.concatenate([mine_ref[...], next_ref[...], rest_ref[...]], axis=0)
    m_high, d_high = matrix.astype(BF), data.astype(BF)
    m_low, d_low = (matrix - m_high.astype(F32)).astype(BF), (data - d_high.astype(F32)).astype(BF)
    out_ref[...] = matmul(m_high, d_high) + matmul(m_high, d_low) + matmul(m_low, d_high)


def spectral_matrices(groups, size):
    points = groups * size
    distance = np.arange(points)[:, None] - np.arange(points)[None, :]
    safe = np.where(distance == 0, 1, distance)
    table = 0.5 * np.where(distance % 2 == 0, 1.0, -1.0) / np.tan(np.pi * safe / points)
    table = np.where(distance == 0, 0.0, table) * FREQUENCY
    out = np.zeros((groups, VROWS, groups * VROWS), np.float32)
    for y in range(groups):
        for row in range(VROWS):
            variable, instance = min(row // size, NV - 1), row % size
            for b in range(groups):
                for t in range(size):
                    column = b * VROWS + size * variable + t
                    out[y, row, column] = table[size * y + instance, size * (y ^ (0, 1, 3, 2)[b]) + t]
    return out


def call(kernel, outputs, scalars, arrays, hbm=0, scratch=(), limit=8):
    smem = pl.BlockSpec(memory_space=pltpu.SMEM)
    vmem = pl.BlockSpec(memory_space=pltpu.VMEM)
    far = pl.BlockSpec(memory_space=pltpu.HBM)
    return pl.pallas_call(
        kernel,
        out_shape=[jax.ShapeDtypeStruct(s, d) for s, d in outputs],
        in_specs=[smem] * len(scalars) + [far] * hbm + [vmem] * (len(arrays) - hbm),
        out_specs=[vmem] * len(outputs),
        scratch_shapes=scratch,
        compiler_params=pltpu.CompilerParams(vmem_limit_bytes=limit << 20),
    )(*scalars, *arrays)


def local(
    state, cell_volume, step_size, face_normal, owner_arm, neighbor_arm, face_owner, face_neighbor, face_count,
    send_cells,
):
    parts = lax.axis_size("dom")
    volume = cell_volume.reshape(1, CELLS)
    step = step_size.reshape(1, CELLS)
    owner = face_owner.reshape(1, FACES)
    neighbor = face_neighbor.reshape(1, FACES)
    matrices = jnp.asarray(spectral_matrices(lax.axis_size("inst"), state.shape[1]))
    inside = [(i, i ^ 1) for i in range(parts)]
    lines = lax.axis_size("inst")
    across = []
    for i in range(parts):
        for y in range(lines):
            j = i + 1 if i % 2 else i - 1
            across.append((lines * i + y, lines * j + y if 0 <= j < parts else lines * i + (y ^ 1)))

    def exchange(near, far, forwarded):
        got = lax.ppermute(near, "dom", inside)
        outgoing = jnp.concatenate([far, got[:forwarded]], axis=0)
        cross = lax.ppermute(outgoing, ("dom", "inst"), across)
        relay = lax.ppermute(cross[: far.shape[0]], "dom", inside)
        return got, cross, relay

    def instances(dense):
        one = lax.ppermute(dense, "inst", [(i, i ^ 1) for i in range(4)])
        outgoing = jnp.concatenate([dense, one], axis=0)
        rest = lax.ppermute(outgoing, "inst", [(i, i ^ 3) for i in range(4)])
        arrays = [matrices, dense, one, rest]
        return call(spectral_kernel, [((VROWS, CELLS), F32)], [], arrays)[0]

    def message(rows):
        return [((rows, 128), F32)] * 2

    dense_shape = ((VROWS, CELLS), F32)
    sources = [pltpu.with_memory_space_constraint(x, pltpu.HBM) for x in (state, send_cells, owner, neighbor)]
    ids = ((1, FACES), jnp.int32)
    near, far, dense, send_hot, owner, neighbor = call(
        send_kernel, message(VROWS) + [dense_shape, ((CELLS, GHOSTS), BF), ids, ids], [], sources, hbm=4,
        scratch=[pltpu.VMEM(state.shape, F32), pltpu.VMEM(send_cells.shape, jnp.int32)] + [pltpu.SemaphoreType.DMA] * 4,
    )
    hot = call(hot_kernel, [((CELLS, FACES), BF), ((CELLS + GHOSTS, FACES), BF)], [], [owner, neighbor])
    for section in range(2):
        jump = call(jump_kernel, [((VROWS, FACES), F32)], [], [dense, *hot])[0]
        ghosts = exchange(near, far, VROWS)
        spectral = instances(dense)
        table, gnear, gfar = call(
            gradient_kernel, [((2 * GROWS, CELLS), BF)] + message(GROWS), [face_count],
            [jump, *ghosts, *hot, face_normal, volume, send_hot],
        )
        arrays = [dense, table, *hot, owner_arm, neighbor_arm]
        face = call(face_kernel, [((8 * NV, FACES), F32)], [], arrays)[0]
        gradient_blocks = exchange(gnear, gfar, GROWS // 2)
        common = [face, *ghosts, *gradient_blocks, *hot, face_normal, neighbor_arm, volume, spectral, step]
        if section == 0:
            dense, near, far = call(
                middle_kernel, [dense_shape] + message(VROWS), [face_count], [*common, dense, send_hot]
            )
    return tuple(call(last_kernel, [(state.shape, F32)] * 2, [face_count], [*common, state]))


def solution(mesh):
    placed = (
        P(None, "inst", "dom"), P("dom"), P("dom"), P(None, "dom"), P(None, "dom"), P(None, "dom"), P("dom"), P("dom"),
        P("dom"), P("dom", None),
    )
    return jax.shard_map(
        local, mesh=mesh, in_specs=placed, out_specs=(P(None, "inst", "dom"), P(None, "inst", "dom")), check_vma=False,
    )
```

time: 50 us -> 49.4 us (0.988)
  no operation moved by 1% of the time
where the time goes in v4:
time: 49.4 us; the launch traced here: 49.3 us
  starting transfers between devices  22 us (45%)
  waiting for transfers between devices  14 us (28%)
  Pallas kernels  11.7 us (24%)
  between operations  1.53 us (3%)
    ppermute x4, starting transfers between devices, exchange(): relay = lax.ppermute(cross[:far.shape[0]], 'dom', inside)  14.5 us
    ppermute x4, waiting for transfers between devices, exchange(): cross = lax.ppermute(outgoing, ('dom', 'inst'), across)  12.5 us
    pallas_call x12, Pallas kernels, call(): pl.pallas_call(kernel, out_shape=[jax.ShapeDtypeStruct(s, d) for s, d in...  11.7 us
    ppermute x2, starting transfers between devices, instances(): rest = lax.ppermute(outgoing, 'inst', [(i, i ^ 3) for i in range(4)])  3.02 us
    ppermute x4, starting transfers between devices, exchange(): cross = lax.ppermute(outgoing, ('dom', 'inst'), across)  1.67 us
    ppermute x2, starting transfers between devices, instances(): one = lax.ppermute(dense, 'inst', [(i, i ^ 1) for i in range(4)])  1.45 us
    ppermute x4, starting transfers between devices, exchange(): got = lax.ppermute(near, 'dom', inside)  1.36 us
    ppermute x4, waiting for transfers between devices, exchange(): got = lax.ppermute(near, 'dom', inside)  1.17 us
  transfers between devices with their start and end apart: 16, of which 7 were waited for; matrix products, arithmetic and copies ran while one was open for 0% of the time, Pallas kernels for 14%

profile of v4, /device:TPU:129, one launch (start us, length us, event | category | flops | bytes accessed | tf_op | source)
XLA Modules:
  0.0 49.3 jit_solution(18149002806792660088)
XLA Ops:
  0.7 1.1 %shard_map.122 = (f32[24,128]{1,0:T(8,128)S(1)}, f32[24,128]{1,0:T(8,128)S(1)}, f32[24,512]{1,0:T(8,128)S(1)}, bf16[512,256]{1,0:T(8,128)(2,1)S(1)}, s32[1,2048]{1,0:T(1,128)S(1)}, /*index=5*/s32[1,2048]{1,0:T(1,128)S(1)}) custom-call(f32[5,4,512]{2,1,0:T(4,128)} %refs_15_.1, s32[4,64]{1,0:T(4,128)} %send_hbm.1, s32[1,2048]{1,0:T(1,128)} %bitcast.10, ...), custom_call_target="tpu_custom_call" | custom-call | tf_op jit(solution)/shard_map/pallas_call | solution.py:277
  1.7 0.8 %collective-permute-start = (f32[24,128]{1,0:T(8,128)S(1)}, f32[24,128]{1,0:T(8,128)S(1)}, u32[]{:S(2)}, u32[]{:S(2)}) collective-permute-start(f32[24,128]{1,0:T(8,128)S(1)} %get-tuple-element.24), channel_id=1, source_target_pairs={{0,4},{4,0},{8,12},{12,8},{16,20},{20,16},{24,28},{28,24},{32,36},... | collective-permute-start | bytes 36872 | tf_op jit(solution)/shard_map/ppermute | solution.py:306
  2.5 1.3 %collective-permute-start.6 = (f32[24,512]{1,0:T(8,128)S(1)}, f32[24,512]{1,0:T(8,128)S(1)}, u32[]{:S(2)}, u32[]{:S(2)}) collective-permute-start(f32[24,512]{1,0:T(8,128)S(1)} %get-tuple-element.19.dense_ref.mine_ref.refs_15_), channel_id=1, source_target_pairs={{0,1},{1,0},{2,3},{3,2},{4,5},{5,4},{6,7},{7,6},{8,9},{9,8},{10,11... | collective-permute-start | bytes 147464 | tf_op jit(solution)/shard_map/ppermute | solution.py:313
  3.8 1.5 %collective-permute-start.1 = (f32[48,128]{1,0:T(8,128)S(1)}, f32[48,128]{1,0:T(8,128)S(1)}, u32[]{:S(2)}, u32[]{:S(2)}) collective-permute-start(f32[48,128]{1,0:T(8,128)S(1)} %pad_maximum_fusion.4), channel_id=1, source_target_pairs={{0,1},{1,0},{2,3},{3,2},{4,8},{5,9},{6,10},{7,11},{8,4},{9,5},{10,... | collective-permute-start | bytes 73736 | tf_op jit(solution)/shard_map/ppermute | solution.py:308
  5.3 1.8 %collective-permute-done.1.cross_in.refs_3_ = f32[48,128]{1,0:T(8,128)S(1)} collective-permute-done((f32[48,128]{1,0:T(8,128)S(1)}, f32[48,128]{1,0:T(8,128)S(1)}, u32[]{:S(2)}, u32[]{:S(2)}) %collective-permute-start.1) | collective-permute-done | bytes 24608 | tf_op jit(solution)/shard_map/ppermute | solution.py:308
  7.0 3.7 %collective-permute-start.2 = (f32[24,128]{1,0:T(8,128)S(1)}, f32[24,128]{1,0:T(8,128)S(1)}, u32[]{:S(2)}, u32[]{:S(2)}) collective-permute-start(f32[24,128]{1,0:T(8,128)S(1)} %slice.24), channel_id=1, source_target_pairs={{0,4},{4,0},{8,12},{12,8},{16,20},{20,16},{24,28},{28,24},{32,36},... | collective-permute-start | bytes 36872 | tf_op jit(solution)/shard_map/ppermute | solution.py:309
  11.4 1.0 %shard_map.123 = (bf16[512,2048]{1,0:T(8,128)(2,1)S(1)}, bf16[768,2048]{1,0:T(8,128)(2,1)S(1)}) custom-call(s32[1,2048]{1,0:T(1,128)S(1)} %get-tuple-element.20.owner_ref, s32[1,2048]{1,0:T(1,128)S(1)} %get-tuple-element.21.neighbor_ref), custom_call_target="tpu_custom_call" | custom-call | tf_op jit(solution)/shard_map/pallas_call | solution.py:277
  12.4 0.5 %shard_map.124.jump_ref = f32[24,2048]{1,0:T(8,128)S(1)} custom-call(f32[24,512]{1,0:T(8,128)S(1)} %get-tuple-element.19.dense_ref.mine_ref.refs_15_, bf16[512,2048]{1,0:T(8,128)(2,1)S(1)} %get-tuple-element.22.own_ref.refs_8_, bf16[768,2048]{1,0:T(8,128)(2,1)S(1)} %get-tuple-element.23.other_ref.refs_9_), custom_call_target="tpu_custom_call" | custom-call | tf_op jit(solution)/shard_map/pallas_call | solution.py:277
  13.0 1.4 %shard_map.125 = (bf16[128,512]{1,0:T(8,128)(2,1)S(1)}, f32[64,128]{1,0:T(8,128)S(1)}, f32[64,128]{1,0:T(8,128)S(1)}) custom-call(s32[1]{0:T(128)S(6)} %copy.13.count_ref.refs_0_, f32[24,2048]{1,0:T(8,128)S(1)} %shard_map.124.jump_ref, f32[24,128]{1,0:T(8,128)S(1)} %collective-permute-done.near_in.refs_2_, ...), custom_call_target="tpu_custom_call" | custom-call | tf_op jit(solution)/shard_map/pallas_call | solution.py:277
  14.5 2.3 %collective-permute-start.7 = (f32[48,512]{1,0:T(8,128)S(1)}, f32[48,512]{1,0:T(8,128)S(1)}, u32[]{:S(2)}, u32[]{:S(2)}) collective-permute-start(f32[48,512]{1,0:T(8,128)S(1)} %pad_maximum_fusion), channel_id=1, source_target_pairs={{0,3},{1,2},{2,1},{3,0},{4,7},{5,6},{6,5},{7,4},{8,11},{9,10},{10,... | collective-permute-start | bytes 294920 | tf_op jit(solution)/shard_map/ppermute | solution.py:315
  16.9 3.7 %collective-permute-done.4.refs_6_ = f32[96,128]{1,0:T(8,128)S(1)} collective-permute-done((f32[96,128]{1,0:T(8,128)S(1)}, f32[96,128]{1,0:T(8,128)S(1)}, u32[]{:S(2)}, u32[]{:S(2)}) %collective-permute-start.4) | collective-permute-done | bytes 49184 | tf_op jit(solution)/shard_map/ppermute | solution.py:308
  20.6 3.9 %collective-permute-start.5 = (f32[64,128]{1,0:T(8,128)S(1)}, f32[64,128]{1,0:T(8,128)S(1)}, u32[]{:S(2)}, u32[]{:S(2)}) collective-permute-start(f32[64,128]{1,0:T(8,128)S(1)} %slice.26), channel_id=1, source_target_pairs={{0,4},{4,0},{8,12},{12,8},{16,20},{20,16},{24,28},{28,24},{32,36},... | collective-permute-start | bytes 98312 | tf_op jit(solution)/shard_map/ppermute | solution.py:309
  24.5 1.0 %shard_map.126.refs_1_ = f32[40,2048]{1,0:T(8,128)S(1)} custom-call(f32[24,512]{1,0:T(8,128)S(1)} %get-tuple-element.19.dense_ref.mine_ref.refs_15_, bf16[128,512]{1,0:T(8,128)(2,1)S(1)} %get-tuple-element.27.table_ref, bf16[512,2048]{1,0:T(8,128)(2,1)S(1)} %get-tuple-element.22.own_ref.refs_8_, bf16[768,2048]{1,0:T(8,128)(2,1)S(1)} %get-tuple-element.23.other_ref.refs_9_, ...), custom_call_target="tpu_custom_call" | custom-call | tf_op jit(solution)/shard_map/pallas_call | solution.py:277
  25.7 1.6 %shard_map.128 = (f32[24,512]{1,0:T(8,128)S(1)}, f32[24,128]{1,0:T(8,128)S(1)}, f32[24,128]{1,0:T(8,128)S(1)}) custom-call(s32[1]{0:T(128)S(6)} %copy.13.count_ref.refs_0_, f32[40,2048]{1,0:T(8,128)S(1)} %shard_map.126.refs_1_, f32[24,128]{1,0:T(8,128)S(1)} %collective-permute-done.near_in.refs_2_, f32[48,128]{1,0:T(8,128)S(1)} %collective-permute-done.1.cross_in.refs_3_, ...), custom_call_target="tpu_custom_call" | custom-call | tf_op jit(solution)/shard_map/pallas_call | solution.py:277
  27.5 1.0 %collective-permute-done.8.near_in.refs_2_ = f32[24,128]{1,0:T(8,128)S(1)} collective-permute-done((f32[24,128]{1,0:T(8,128)S(1)}, f32[24,128]{1,0:T(8,128)S(1)}, u32[]{:S(2)}, u32[]{:S(2)}) %collective-permute-start.8) | collective-permute-done | bytes 12320 | tf_op jit(solution)/shard_map/ppermute | solution.py:306
  28.6 3.2 %collective-permute-done.9.cross_in.refs_3_ = f32[48,128]{1,0:T(8,128)S(1)} collective-permute-done((f32[48,128]{1,0:T(8,128)S(1)}, f32[48,128]{1,0:T(8,128)S(1)}, u32[]{:S(2)}, u32[]{:S(2)}) %collective-permute-start.9) | collective-permute-done | bytes 24608 | tf_op jit(solution)/shard_map/ppermute | solution.py:308
  31.8 3.5 %collective-permute-start.10 = (f32[24,128]{1,0:T(8,128)S(1)}, f32[24,128]{1,0:T(8,128)S(1)}, u32[]{:S(2)}, u32[]{:S(2)}) collective-permute-start(f32[24,128]{1,0:T(8,128)S(1)} %slice.27), channel_id=1, source_target_pairs={{0,4},{4,0},{8,12},{12,8},{16,20},{20,16},{24,28},{28,24},{32,36},... | collective-permute-start | bytes 36872 | tf_op jit(solution)/shard_map/ppermute | solution.py:309
  35.3 0.5 %shard_map.129.jump_ref = f32[24,2048]{1,0:T(8,128)S(1)} custom-call(f32[24,512]{1,0:T(8,128)S(1)} %get-tuple-element.30.dense_ref.mine_ref, bf16[512,2048]{1,0:T(8,128)(2,1)S(1)} %get-tuple-element.22.own_ref.refs_8_, bf16[768,2048]{1,0:T(8,128)(2,1)S(1)} %get-tuple-element.23.other_ref.refs_9_), custom_call_target="tpu_custom_call" | custom-call | tf_op jit(solution)/shard_map/pallas_call | solution.py:277
  36.1 1.4 %shard_map.130 = (bf16[128,512]{1,0:T(8,128)(2,1)S(1)}, f32[64,128]{1,0:T(8,128)S(1)}, f32[64,128]{1,0:T(8,128)S(1)}) custom-call(s32[1]{0:T(128)S(6)} %copy.13.count_ref.refs_0_, f32[24,2048]{1,0:T(8,128)S(1)} %shard_map.129.jump_ref, f32[24,128]{1,0:T(8,128)S(1)} %collective-permute-done.8.near_in.refs_2_, ...), custom_call_target="tpu_custom_call" | custom-call | tf_op jit(solution)/shard_map/pallas_call | solution.py:277
  37.9 0.7 %collective-permute-start.15 = (f32[48,512]{1,0:T(8,128)S(1)}, f32[48,512]{1,0:T(8,128)S(1)}, u32[]{:S(2)}, u32[]{:S(2)}) collective-permute-start(f32[48,512]{1,0:T(8,128)S(1)} %pad_maximum_fusion.1), channel_id=1, source_target_pairs={{0,3},{1,2},{2,1},{3,0},{4,7},{5,6},{6,5},{7,4},{8,11},{9,10},{10,... | collective-permute-start | bytes 294920 | tf_op jit(solution)/shard_map/ppermute | solution.py:315
  38.9 3.8 %collective-permute-done.12.refs_6_ = f32[96,128]{1,0:T(8,128)S(1)} collective-permute-done((f32[96,128]{1,0:T(8,128)S(1)}, f32[96,128]{1,0:T(8,128)S(1)}, u32[]{:S(2)}, u32[]{:S(2)}) %collective-permute-start.12) | collective-permute-done | bytes 49184 | tf_op jit(solution)/shard_map/ppermute | solution.py:308
  42.7 3.4 %collective-permute-start.13 = (f32[64,128]{1,0:T(8,128)S(1)}, f32[64,128]{1,0:T(8,128)S(1)}, u32[]{:S(2)}, u32[]{:S(2)}) collective-permute-start(f32[64,128]{1,0:T(8,128)S(1)} %slice.29), channel_id=1, source_target_pairs={{0,4},{4,0},{8,12},{12,8},{16,20},{20,16},{24,28},{28,24},{32,36},... | collective-permute-start | bytes 98312 | tf_op jit(solution)/shard_map/ppermute | solution.py:309
  46.0 1.0 %shard_map.131.refs_1_ = f32[40,2048]{1,0:T(8,128)S(1)} custom-call(f32[24,512]{1,0:T(8,128)S(1)} %get-tuple-element.30.dense_ref.mine_ref, bf16[128,512]{1,0:T(8,128)(2,1)S(1)} %get-tuple-element.33.table_ref, bf16[512,2048]{1,0:T(8,128)(2,1)S(1)} %get-tuple-element.22.own_ref.refs_8_, bf16[768,2048]{1,0:T(8,128)(2,1)S(1)} %get-tuple-element.23.other_ref.refs_9_, ...), custom_call_target="tpu_custom_call" | custom-call | tf_op jit(solution)/shard_map/pallas_call | solution.py:277
  47.2 2.1 %shard_map.133 = (f32[5,4,512]{2,1,0:T(4,128)}, f32[5,4,512]{2,1,0:T(4,128)}) custom-call(s32[1]{0:T(128)S(6)} %copy.13.count_ref.refs_0_, f32[40,2048]{1,0:T(8,128)S(1)} %shard_map.131.refs_1_, f32[24,128]{1,0:T(8,128)S(1)} %collective-permute-done.8.near_in.refs_2_, f32[48,128]{1,0:T(8,128)S(1)} %collective-permute-done.9.cross_in.refs_3_, ...), custom_call_target="tpu_custom_call" | custom-call | tf_op jit(solution)/shard_map/pallas_call | solution.py:277
  (46 shorter events, 1.9 us)
Async XLA Ops:
  0.6 12.3 %copy-start = (f32[3,2048]{1,0:T(4,128)S(1)}, f32[3,2048]{1,0:T(4,128)}, u32[]{:S(2)}) copy-start(f32[3,2048]{1,0:T(4,128)} %refs_10_.3) | copy-start | bytes 73732
  0.6 12.3 %copy-start.5 = (f32[512]{0:T(512)S(1)}, f32[512]{0:T(512)}, u32[]{:S(2)}) copy-start(f32[512]{0:T(512)} %param.12) | copy-start | bytes 6148
  1.7 2.1 %collective-permute-start = (f32[24,128]{1,0:T(8,128)S(1)}, f32[24,128]{1,0:T(8,128)S(1)}, u32[]{:S(2)}, u32[]{:S(2)}) collective-permute-start(f32[24,128]{1,0:T(8,128)S(1)} %get-tuple-element.24), channel_id=1, source_target_pairs={{0,4},{4,0},{8,12},{12,8},{16,20},{20,16},{24,28},{28,24},{32,36},... | collective-permute-start | bytes 36872 | tf_op jit(solution)/shard_map/ppermute | solution.py:306
  2.5 12.0 %collective-permute-start.6 = (f32[24,512]{1,0:T(8,128)S(1)}, f32[24,512]{1,0:T(8,128)S(1)}, u32[]{:S(2)}, u32[]{:S(2)}) collective-permute-start(f32[24,512]{1,0:T(8,128)S(1)} %get-tuple-element.19.dense_ref.mine_ref.refs_15_), channel_id=1, source_target_pairs={{0,1},{1,0},{2,3},{3,2},{4,5},{5,4},{6,7},{7,6},{8,9},{9,8},{10,11... | collective-permute-start | bytes 147464 | tf_op jit(solution)/shard_map/ppermute | solution.py:313
  3.8 3.3 %collective-permute-start.1 = (f32[48,128]{1,0:T(8,128)S(1)}, f32[48,128]{1,0:T(8,128)S(1)}, u32[]{:S(2)}, u32[]{:S(2)}) collective-permute-start(f32[48,128]{1,0:T(8,128)S(1)} %pad_maximum_fusion.4), channel_id=1, source_target_pairs={{0,1},{1,0},{2,3},{3,2},{4,8},{5,9},{6,10},{7,11},{8,4},{9,5},{10,... | collective-permute-start | bytes 73736 | tf_op jit(solution)/shard_map/ppermute | solution.py:308
  7.0 5.9 %collective-permute-start.2 = (f32[24,128]{1,0:T(8,128)S(1)}, f32[24,128]{1,0:T(8,128)S(1)}, u32[]{:S(2)}, u32[]{:S(2)}) collective-permute-start(f32[24,128]{1,0:T(8,128)S(1)} %slice.24), channel_id=1, source_target_pairs={{0,4},{4,0},{8,12},{12,8},{16,20},{20,16},{24,28},{28,24},{32,36},... | collective-permute-start | bytes 36872 | tf_op jit(solution)/shard_map/ppermute | solution.py:309
  12.9 11.6 %copy-start.1 = (f32[3,2048]{1,0:T(4,128)S(1)}, f32[3,2048]{1,0:T(4,128)}, u32[]{:S(2)}) copy-start(f32[3,2048]{1,0:T(4,128)} %refs_11_.3) | copy-start | bytes 73732
  12.9 11.6 %copy-start.4 = (f32[3,2048]{1,0:T(4,128)S(1)}, f32[3,2048]{1,0:T(4,128)}, u32[]{:S(2)}) copy-start(f32[3,2048]{1,0:T(4,128)} %owner_arm_ref.3) | copy-start | bytes 73732
  14.4 11.2 %copy-start.2 = (f32[4,24,96]{2,1,0:T(8,128)S(1)}, f32[4,24,96]{2,1,0:T(8,128)}, u32[]{:S(2)}) copy-start(f32[4,24,96]{2,1,0:T(8,128)} %constant.2.clone.matrix_ref) | copy-start | bytes 110596
  14.4 2.5 %collective-permute-start.3 = (f32[64,128]{1,0:T(8,128)S(1)}, f32[64,128]{1,0:T(8,128)S(1)}, u32[]{:S(2)}, u32[]{:S(2)}) collective-permute-start(f32[64,128]{1,0:T(8,128)S(1)} %get-tuple-element.28), channel_id=1, source_target_pairs={{0,4},{4,0},{8,12},{12,8},{16,20},{20,16},{24,28},{28,24},{32,36},... | collective-permute-start | bytes 98312 | tf_op jit(solution)/shard_map/ppermute | solution.py:306
  14.5 11.0 %collective-permute-start.7 = (f32[48,512]{1,0:T(8,128)S(1)}, f32[48,512]{1,0:T(8,128)S(1)}, u32[]{:S(2)}, u32[]{:S(2)}) collective-permute-start(f32[48,512]{1,0:T(8,128)S(1)} %pad_maximum_fusion), channel_id=1, source_target_pairs={{0,3},{1,2},{2,1},{3,0},{4,7},{5,6},{6,5},{7,4},{8,11},{9,10},{10,... | collective-permute-start | bytes 294920 | tf_op jit(solution)/shard_map/ppermute | solution.py:315
  16.8 8.9 %copy-start.6 = (f32[512]{0:T(512)S(1)}, f32[512]{0:T(512)}, u32[]{:S(2)}) copy-start(f32[512]{0:T(512)} %param.13) | copy-start | bytes 6148
  16.8 3.8 %collective-permute-start.4 = (f32[96,128]{1,0:T(8,128)S(1)}, f32[96,128]{1,0:T(8,128)S(1)}, u32[]{:S(2)}, u32[]{:S(2)}) collective-permute-start(f32[96,128]{1,0:T(8,128)S(1)} %pad_maximum_fusion.2), channel_id=1, source_target_pairs={{0,1},{1,0},{2,3},{3,2},{4,8},{5,9},{6,10},{7,11},{8,4},{9,5},{10,... | collective-permute-start | bytes 147464 | tf_op jit(solution)/shard_map/ppermute | solution.py:308
  20.6 5.1 %collective-permute-start.5 = (f32[64,128]{1,0:T(8,128)S(1)}, f32[64,128]{1,0:T(8,128)S(1)}, u32[]{:S(2)}, u32[]{:S(2)}) collective-permute-start(f32[64,128]{1,0:T(8,128)S(1)} %slice.26), channel_id=1, source_target_pairs={{0,4},{4,0},{8,12},{12,8},{16,20},{20,16},{24,28},{28,24},{32,36},... | collective-permute-start | bytes 98312 | tf_op jit(solution)/shard_map/ppermute | solution.py:309
  27.3 1.3 %collective-permute-start.8 = (f32[24,128]{1,0:T(8,128)S(1)}, f32[24,128]{1,0:T(8,128)S(1)}, u32[]{:S(2)}, u32[]{:S(2)}) collective-permute-start(f32[24,128]{1,0:T(8,128)S(1)} %get-tuple-element.31), channel_id=1, source_target_pairs={{0,4},{4,0},{8,12},{12,8},{16,20},{20,16},{24,28},{28,24},{32,36},... | collective-permute-start | bytes 36872 | tf_op jit(solution)/shard_map/ppermute | solution.py:306
  27.4 10.5 %collective-permute-start.14 = (f32[24,512]{1,0:T(8,128)S(1)}, f32[24,512]{1,0:T(8,128)S(1)}, u32[]{:S(2)}, u32[]{:S(2)}) collective-permute-start(f32[24,512]{1,0:T(8,128)S(1)} %get-tuple-element.30.dense_ref.mine_ref), channel_id=1, source_target_pairs={{0,1},{1,0},{2,3},{3,2},{4,5},{5,4},{6,7},{7,6},{8,9},{9,8},{10,11... | collective-permute-start | bytes 147464 | tf_op jit(solution)/shard_map/ppermute | solution.py:313
  28.5 3.3 %collective-permute-start.9 = (f32[48,128]{1,0:T(8,128)S(1)}, f32[48,128]{1,0:T(8,128)S(1)}, u32[]{:S(2)}, u32[]{:S(2)}) collective-permute-start(f32[48,128]{1,0:T(8,128)S(1)} %pad_maximum_fusion.5), channel_id=1, source_target_pairs={{0,1},{1,0},{2,3},{3,2},{4,8},{5,9},{6,10},{7,11},{8,4},{9,5},{10,... | collective-permute-start | bytes 73736 | tf_op jit(solution)/shard_map/ppermute | solution.py:308
  31.8 4.3 %collective-permute-start.10 = (f32[24,128]{1,0:T(8,128)S(1)}, f32[24,128]{1,0:T(8,128)S(1)}, u32[]{:S(2)}, u32[]{:S(2)}) collective-permute-start(f32[24,128]{1,0:T(8,128)S(1)} %slice.27), channel_id=1, source_target_pairs={{0,4},{4,0},{8,12},{12,8},{16,20},{20,16},{24,28},{28,24},{32,36},... | collective-permute-start | bytes 36872 | tf_op jit(solution)/shard_map/ppermute | solution.py:309
  37.5 1.3 %collective-permute-start.11 = (f32[64,128]{1,0:T(8,128)S(1)}, f32[64,128]{1,0:T(8,128)S(1)}, u32[]{:S(2)}, u32[]{:S(2)}) collective-permute-start(f32[64,128]{1,0:T(8,128)S(1)} %get-tuple-element.34), channel_id=1, source_target_pairs={{0,4},{4,0},{8,12},{12,8},{16,20},{20,16},{24,28},{28,24},{32,36},... | collective-permute-start | bytes 98312 | tf_op jit(solution)/shard_map/ppermute | solution.py:306
  37.9 9.1 %collective-permute-start.15 = (f32[48,512]{1,0:T(8,128)S(1)}, f32[48,512]{1,0:T(8,128)S(1)}, u32[]{:S(2)}, u32[]{:S(2)}) collective-permute-start(f32[48,512]{1,0:T(8,128)S(1)} %pad_maximum_fusion.1), channel_id=1, source_target_pairs={{0,3},{1,2},{2,1},{3,0},{4,7},{5,6},{6,5},{7,4},{8,11},{9,10},{10,... | collective-permute-start | bytes 294920 | tf_op jit(solution)/shard_map/ppermute | solution.py:315
  38.8 8.5 %copy-start.3 = (f32[5,4,512]{2,1,0:T(4,128)S(1)}, f32[5,4,512]{2,1,0:T(4,128)}, u32[]{:S(2)}) copy-start(f32[5,4,512]{2,1,0:T(4,128)} %refs_15_.1) | copy-start | bytes 122884
  38.8 3.9 %collective-permute-start.12 = (f32[96,128]{1,0:T(8,128)S(1)}, f32[96,128]{1,0:T(8,128)S(1)}, u32[]{:S(2)}, u32[]{:S(2)}) collective-permute-start(f32[96,128]{1,0:T(8,128)S(1)} %pad_maximum_fusion.3), channel_id=1, source_target_pairs={{0,1},{1,0},{2,3},{3,2},{4,8},{5,9},{6,10},{7,11},{8,4},{9,5},{10,... | collective-permute-start | bytes 147464 | tf_op jit(solution)/shard_map/ppermute | solution.py:308
  42.7 4.5 %collective-permute-start.13 = (f32[64,128]{1,0:T(8,128)S(1)}, f32[64,128]{1,0:T(8,128)S(1)}, u32[]{:S(2)}, u32[]{:S(2)}) collective-permute-start(f32[64,128]{1,0:T(8,128)S(1)} %slice.29), channel_id=1, source_target_pairs={{0,4},{4,0},{8,12},{12,8},{16,20},{20,16},{24,28},{28,24},{32,36},... | collective-permute-start | bytes 98312 | tf_op jit(solution)/shard_map/ppermute | solution.py:309
